TPU v7x, 32 devices: a whole 2x2x4 slice. The times are simulated.
32 devices in a mesh: depth: 16 (over z, y, x), light: 2 (over core).
Axes of the slice: x: 2, y: 2, z: 4, core: 2. Of those that a mesh axis runs over, the one named last changes fastest.
Arguments:
- density: float32 [64, 128, 1024], P('depth', 'light'), may hold values from -6 to 6
- labels: int32 [64, 128, 1024], P('depth', 'light'), may hold values from 0 to 15
- slice_order: int32 [64], P('depth'), may hold values from 0 to 63, as said below
- extinction: float32 [16], replicated, may hold values from 0.0001 to 0.01
- albedo: float32 [3, 16], replicated, may hold values from 0.2 to 1
Outputs:
- image: float32 [4, 131072], P(None, ('light', 'depth'))
Inputs may be any that keep to these rules, and one draw needn't show every extreme that they name: Within each aligned block of 4 view positions, slice_order is a permutation of that block's positions.
All inputs are finite; a program needn't handle non-finite values.
Results may differ from a plain program's by a relative error of at most 0.0003.
Values sent between devices are 32-bit elements; how exact they have to be, the bound alone decides.
A program may use at most 64 MiB of HBM per device.

v0:
```python
import jax
import jax.numpy as jnp
from jax import lax
from jax.sharding import PartitionSpec as P


def padded_2(cells, sides, width):
    for axis, dim in sides:
        count = lax.axis_size(axis)
        ends = count - 1
        head = lax.slice_in_dim(cells, 0, width, axis=dim)
        tail = lax.slice_in_dim(cells, cells.shape[dim] - width, cells.shape[dim], axis=dim)
        cells = jnp.concatenate(
            [
                lax.ppermute(tail, axis, [(i, (i + 1) % count) for i in range(ends)]),
                cells,
                lax.ppermute(head, axis, [((i + 1) % count, i) for i in range(ends)]),
            ],
            axis=dim,
        )
    return cells


def entering(part, axis, combine, identity):
    place = lax.axis_index(axis)
    gathered = lax.all_gather(part, axis)
    state = jnp.zeros_like(part) + jnp.asarray(identity, part.dtype)

    def one(step, state):
        return combine(state, lax.dynamic_index_in_dim(gathered, step, 0, False))

    return lax.fori_loop(0, place, one, state)


def partner(block, axis, stride):
    count = lax.axis_size(axis)
    route = []
    for low in range(count):
        high = low | 1 << stride
        if high != low and high < count:
            route += [(low, high), (high, low)]
    return lax.ppermute(block, axis, route)


def smooth_field(padded):
    center = padded[1:-1, 1:-1, 1:-1]
    beside = padded[2:, 1:-1, 1:-1] + padded[:-2, 1:-1, 1:-1]
    beside = beside + padded[1:-1, 2:, 1:-1] + padded[1:-1, :-2, 1:-1]
    beside = beside + padded[1:-1, 1:-1, 2:] + padded[1:-1, 1:-1, :-2]
    return 0.4 * center + 0.1 * beside


def gradient_parts(padded):
    center = padded[1:-1, 1:-1, 1:-1]
    grad_z = 0.5 * (padded[2:, 1:-1, 1:-1] - padded[:-2, 1:-1, 1:-1])
    grad_x = 0.5 * (padded[1:-1, 2:, 1:-1] - padded[1:-1, :-2, 1:-1])
    grad_y = 0.5 * (padded[1:-1, 1:-1, 2:] - padded[1:-1, 1:-1, :-2])
    return (center, grad_z, grad_x, grad_y)


def material_props(materials, extinction, albedo):
    lookup_table = jnp.concatenate([extinction[None, :], albedo], axis=0)
    result = jnp.zeros((4,) + materials.shape, jnp.float32)
    for number in range(lookup_table.shape[1]):
        result = jnp.where(
            materials[None] == number, lookup_table[:, number][:, None, None, None], result
        )
    return result


def over_blend(front_part, back_part):
    return front_part + (1.0 - front_part[3:4]) * back_part


def shards(density, labels, slice_order, extinction, albedo):
    depth_count = lax.axis_size("depth")
    light_count = lax.axis_size("light")
    depth_at = lax.axis_index("depth")
    light_at = lax.axis_index("light")
    slices, x_cells, y_rows = density.shape
    local_order = slice_order % slices
    viewed = jnp.take(density, local_order, axis=0)
    materials = jnp.take(labels, local_order, axis=0)
    wide_rim = padded_2(viewed, (("depth", 0), ("light", 1)), 2)
    smoothed = smooth_field(jnp.pad(wide_rim, ((0, 0), (0, 0), (2, 2))))
    z_pos = jnp.arange(slices + 2, dtype=jnp.int32) - 1 + depth_at * slices
    x_pos = jnp.arange(x_cells + 2, dtype=jnp.int32) - 1 + light_at * x_cells
    y_pos = jnp.arange(y_rows + 2, dtype=jnp.int32)
    inside_z = (z_pos >= 0) & (z_pos < slices * depth_count)
    inside_x = (x_pos >= 0) & (x_pos < x_cells * light_count)
    inside_y = (y_pos >= 1) & (y_pos <= y_rows)
    keep_mask = inside_z[:, None, None] & inside_x[None, :, None] & inside_y[None, None, :]
    second = jnp.where(keep_mask, smoothed, jnp.float32(0.0))
    center, grad_z, grad_x, grad_y = gradient_parts(second)
    material = material_props(materials, extinction, albedo)
    optical = material[0] * jnp.exp(center)
    cell_ids = jnp.arange(x_cells, dtype=jnp.int32)
    earlier_cells = (cell_ids[:, None] < cell_ids[None, :]).astype(jnp.float32)
    light_sum = jnp.einsum("zwy,wx->zxy", optical, earlier_cells, precision=lax.Precision.HIGHEST)
    through = jnp.exp(-jnp.sum(optical, axis=1))
    incoming = entering(
        through,
        "light",
        lambda earlier_part, later_part: earlier_part * later_part,
        jnp.ones_like(through),
    )
    lighted = jnp.exp(-light_sum) * incoming[:, None, :]
    opacity = 1.0 - jnp.exp(-optical)
    facing = grad_x / jnp.sqrt(grad_z * grad_z + grad_x * grad_x + grad_y * grad_y + 0.05)
    shading = 0.2 + lighted * (0.5 + 0.5 * facing)
    depth_total = jnp.cumsum(optical, axis=0)
    depth_before = jnp.concatenate([jnp.zeros_like(optical[:1]), depth_total[:-1]], axis=0)
    weight = opacity * shading * jnp.exp(-depth_before)
    colour = jnp.sum(material[1:] * weight[None], axis=1)
    coverage = 1.0 - jnp.exp(-jnp.sum(optical, axis=0))
    partial_value = jnp.concatenate([colour, coverage[None]], axis=0).reshape(4, depth_count, -1)
    current = partial_value
    for bit_number in range(depth_count.bit_length() - 1):
        blocks = current.shape[1]
        halves = current.reshape(4, blocks // 2, 2, current.shape[2])
        upper_bit = depth_at >> bit_number & 1
        kept_half = lax.dynamic_index_in_dim(halves, upper_bit, 2, False)
        given_half = lax.dynamic_index_in_dim(halves, 1 - upper_bit, 2, False)
        taken_half = partner(given_half, "depth", bit_number)
        in_front = jnp.where(upper_bit == 0, kept_half, taken_half)
        behind = jnp.where(upper_bit == 0, taken_half, kept_half)
        current = over_blend(in_front, behind)
    return current.reshape(4, -1)


def solution(mesh):
    return jax.shard_map(
        shards,
        mesh=mesh,
        in_specs=(P("depth", "light", None), P("depth", "light", None), P("depth"), P(), P()),
        out_specs=P(None, ("light", "depth")),
        check_vma=False,
    )
```

profile of v0, /device:TPU:24, one launch (start us, length us, event | category | flops | bytes accessed | tf_op | source)
XLA Modules:
  0.0 93.1 jit_solution(5435525948337167428)
XLA Ops:
  0.0 0.8 compare_and_fusion.2
  1.2 0.6 gather_fusion.1
  2.1 1.1 %fusion.38 = (f32[2,64,1024]{2,1,0:T(8,128)}, f32[2,64,1024]{2,1,0:T(8,128)}) fusion(f32[4,64,1024]{2,1,0:T(8,128)S(1)} %broadcast_select_fusion), kind=kLoop, calls=%fused_computation.133 | loop fusion | bytes 2097152 | tf_op jit(solution)/shard_map/slice | solution.py:12
  3.1 3.4 %collective-permute-start = (f32[2,64,1024]{2,1,0:T(8,128)}, f32[2,64,1024]{2,1,0:T(8,128)}, u32[]{:S(2)}, u32[]{:S(2)}) collective-permute-start(f32[2,64,1024]{2,1,0:T(8,128)} %get-tuple-element.78), channel_id=1, source_target_pairs={{0,2},{2,4},{4,6},{6,8},{8,10},{10,12},{12,14},{14,16},{16,18},{18... | collective-permute-start | bytes 1572872 | tf_op jit(solution)/shard_map/ppermute | solution.py:15
  6.5 4.2 %collective-permute-start.1 = (f32[2,64,1024]{2,1,0:T(8,128)}, f32[2,64,1024]{2,1,0:T(8,128)}, u32[]{:S(2)}, u32[]{:S(2)}) collective-permute-start(f32[2,64,1024]{2,1,0:T(8,128)} %get-tuple-element.79), channel_id=1, source_target_pairs={{2,0},{4,2},{6,4},{8,6},{10,8},{12,10},{14,12},{16,14},{18,16},{20... | collective-permute-start | bytes 1572872 | tf_op jit(solution)/shard_map/ppermute | solution.py:17
  10.8 1.8 %gather_fusion = s32[4,64,1024]{2,1,0:T(8,128)S(1)} fusion(s32[4,64,1024]{2,1,0:T(8,128)} %param.8, s32[1024]{0:T(1024)S(1)} %pad_clamp_fusion), kind=kCustom, calls=%fused_computation | custom fusion | bytes 2097168 | tf_op jit(solution)/shard_map/jit(_take)/gather | solution.py:83
  12.7 2.9 %broadcast_compare_fusion.15 = (pred[4,64,1024]{2,1,0:T(8,128)(4,1)S(1)}, pred[4,64,1024]{2,1,0:T(8,128)(4,1)S(1)}, pred[4,64,1024]{2,1,0:T(8,128)(4,1)S(1)}, pr...) fusion(s32[4,64,1024]{2,1,0:T(8,128)S(1)} %gather_fusion, ...), kind=kLoop, calls=%fused_computation.69 | loop fusion | flops 4456448 | bytes 5242884 | tf_op jit(solution)/shard_map/eq | solution.py:66
  16.0 7.0 %select_select_fusion = f32[4,4,64,1024]{3,2,1,0:T(8,128)} fusion(f32[4]{0:T(128)S(1)} %get-tuple-element.32, f32[4]{0:T(128)S(1)} %get-tuple-element.33, f32[4]{0:T(128)S(1)} %get-tuple-element.34, f32[4]{0:T(128)S(1)} %get-tuple-element.35, f32[4]{0:T(128)S(1)} %get-tuple-element.36, f32[4]{0:T(128)S(1)} %get-tuple-element.37, f32[4]{0:T(128)S(1)} %get-tuple-element.38, ...), kind=kLoop, calls=%fused_computation.3 | loop fusion | flops 16777216 | bytes 8388864 | tf_op jit(solution)/shard_map/jit(_where)/select_n | solution.py:65
  23.1 8.0 %collective-permute-done.1 = f32[2,64,1024]{2,1,0:T(8,128)} collective-permute-done((f32[2,64,1024]{2,1,0:T(8,128)}, f32[2,64,1024]{2,1,0:T(8,128)}, u32[]{:S(2)}, u32[]{:S(2)}) %collective-permute-start.1) | collective-permute-done | bytes 524320 | tf_op jit(solution)/shard_map/ppermute | solution.py:17
  31.2 1.0 %pad_maximum_fusion.2 = (f32[8,2,1024]{2,1,0:T(2,128)S(1)}, f32[8,2,1024]{2,1,0:T(2,128)S(1)}) fusion(f32[2,64,1024]{2,1,0:T(8,128)} %collective-permute-done.1, f32[4,64,1024]{2,1,0:T(8,128)S(1)} %broadcast_select_fusion, f32[2,64,1024]{2,1,0:T(8,128)} %collective-permute-done), kind=kLoop, calls=%fused_computation.87 | loop fusion | flops 65536 | bytes 2228224 | tf_op jit(solution)/shard_map/slice | solution.py:12
  32.2 1.3 %collective-permute-start.2 = (f32[8,2,1024]{2,1,0:T(2,128)S(1)}, f32[8,2,1024]{2,1,0:T(2,128)S(1)}, u32[]{:S(2)}, u32[]{:S(2)}) collective-permute-start(f32[8,2,1024]{2,1,0:T(2,128)S(1)} %get-tuple-element.58), channel_id=1, source_target_pairs={{0,1},{2,3},{4,5},{6,7},{8,9},{10,11},{12,13},{14,15},{16,17},{18,... | collective-permute-start | bytes 196616 | tf_op jit(solution)/shard_map/ppermute | solution.py:15
  33.5 1.3 %collective-permute-start.3 = (f32[8,2,1024]{2,1,0:T(2,128)S(1)}, f32[8,2,1024]{2,1,0:T(2,128)S(1)}, u32[]{:S(2)}, u32[]{:S(2)}) collective-permute-start(f32[8,2,1024]{2,1,0:T(2,128)S(1)} %get-tuple-element.59), channel_id=1, source_target_pairs={{1,0},{3,2},{5,4},{7,6},{9,8},{11,10},{13,12},{15,14},{17,16},{19,... | collective-permute-start | bytes 196616 | tf_op jit(solution)/shard_map/ppermute | solution.py:17
  34.8 1.8 %collective-permute-done.3 = f32[8,2,1024]{2,1,0:T(2,128)S(1)} collective-permute-done((f32[8,2,1024]{2,1,0:T(2,128)S(1)}, f32[8,2,1024]{2,1,0:T(2,128)S(1)}, u32[]{:S(2)}, u32[]{:S(2)}) %collective-permute-start.3) | collective-permute-done | bytes 65568 | tf_op jit(solution)/shard_map/ppermute | solution.py:17
  36.6 2.2 %select_maximum_fusion = f32[8,68,1028]{2,1,0:T(8,128)S(1)} fusion(f32[8,2,1024]{2,1,0:T(2,128)S(1)} %collective-permute-done.3, f32[8,2,1024]{2,1,0:T(2,128)S(1)} %collective-permute-done.2, f32[2,64,1024]{2,1,0:T(8,128)} %collective-permute-done.1, f32[4,64,1024]{2,1,0:T(8,128)S(1)} %broadcast_select_fusion, f32[2,64,1024]{2,1,0:T(8,128)} %collective-permute-done), kind=kLoop, calls=%fused_computation.8 | loop fusion | flops 6710784 | bytes 4465152 | tf_op jit(solution)/shard_map/concatenate | solution.py:13
  38.8 3.4 %fusion.4 = f32[6,66,1026]{2,1,0:T(8,128)S(1)} fusion(f32[8,68,1028]{2,1,0:T(8,128)S(1)} %select_maximum_fusion, pred[1026]{0:T(1024)(128)(4,1)S(1)} %fusion.34, pred[6,66]{1,0:T(8,128)(4,1)S(1)} %broadcast_and_fusion), kind=kLoop, calls=%fused_computation.16 | loop fusion | flops 4062960 | bytes 13002894 | tf_op jit(solution)/shard_map/jit(_where)/select_n | solution.py:93
  42.2 2.4 %fusion.36 = (f32[64,1024]{1,0:T(8,128)}, f32[4,1024]{1,0:T(4,128)S(1)}, f32[4,64,1024]{2,1,0:T(8,128)S(1)}) fusion(f32[6,66,1026]{2,1,0:T(8,128)S(1)} %fusion.4, f32[4,4,64,1024]{3,2,1,0:T(8,128)} %select_select_fusion), kind=kLoop, calls=%fused_computation.132 | loop fusion | flops 716800 | bytes 3424256 | tf_op jit(solution)/shard_map/reduce_sum | solution.py:115
  44.6 1.0 %copy-done.2 = f32[4,64,1024]{2,1,0:T(8,128)} copy-done((f32[4,64,1024]{2,1,0:T(8,128)}, f32[4,64,1024]{2,1,0:T(8,128)S(1)}, u32[]{:S(2)}) %copy-start.2) | copy-done | bytes 1048600
  45.6 1.2 %fusion.39 = f32[4,64,1024]{2,1,0:T(8,128)S(1)} fusion(f32[4,64,1024]{2,1,0:T(8,128)S(1)} %get-tuple-element.55), kind=kOutput, calls=%fused_computation.134 | output fusion | flops 786432 | bytes 2097152 | tf_op jit(solution)/shard_map/jit(cumsum)/reduce_window_sum | solution.py:111
  46.8 1.0 %slice.186 = f32[3,64,1024]{2,1,0:T(8,128)} slice(f32[4,64,1024]{2,1,0:T(8,128)S(1)} %fusion.39), slice={[0:3], [0:64], [0:1024]} | slice | bytes 1572864 | tf_op jit(solution)/shard_map/slice | solution.py:112
  47.8 1.8 %all-gather.1 = f32[2,4,1024]{2,1,0:T(4,128)S(1)} all-gather(f32[1,4,1024]{2,1,0:T(4,128)S(1)} %exponential_bitcast_fusion), channel_id=2, replica_groups=mesh['depth'=16,'light'=2] {'light'}, dimensions={0}, use_global_device_ids=true | all-gather | bytes 49152 | tf_op jit(solution)/shard_map/all_gather | solution.py:26
  49.9 4.1 %fusion.11 = f32[4,64,1024]{2,1,0:T(8,128)S(1)} fusion(f32[4,64,1024]{2,1,0:T(8,128)} %copy-done.2, f32[6,66,1026]{2,1,0:T(8,128)S(1)} %fusion.4, f32[3,64,1024]{2,1,0:T(8,128)} %slice.186, f32[4,1024]{1,0:T(4,128)S(1)} %get-tuple-element.28), kind=kOutput, calls=%fused_computation.29 | convolution fusion | flops 207622144 | bytes 10240000 | tf_op jit(solution)/shard_map/zwy,wx->zxy/dot_general | solution.py:99
  54.0 0.5 fusion
  54.6 0.6 concatenate.22
  55.3 1.0 %exponential_subtract_fusion = f32[64,1024]{1,0:T(8,128)S(1)} fusion(f32[64,1024]{1,0:T(8,128)} %get-tuple-element.29), kind=kLoop, calls=%fused_computation.76 | loop fusion | flops 131072 | bytes 524288 | tf_op jit(solution)/shard_map/sub | solution.py:115
  56.5 1.1 %constant_dynamic-slice_fusion.2 = (f32[4,8,1,4096]{3,2,1,0:T(1,128)S(1)}, f32[4,8,1,4096]{3,2,1,0:T(1,128)S(1)}) fusion(f32[4,8,2,4096]{3,2,1,0:T(2,128)S(1)} %constant_dynamic-update-slice_fusion, s32[]{:T(128)S(6)} %select_n.229, s32[]{:T(128)S(6)} %select_n.230), kind=kLoop, calls=%fused_computation.125 | loop fusion | bytes 2097160 | tf_op jit(solution)/shard_map/jit(dynamic_index_in_dim)/dynamic_slice | solution.py:122
  57.9 1.6 %collective-permute-start.4 = (f32[4,8,4096]{2,1,0:T(8,128)S(1)}, f32[4,8,4096]{2,1,0:T(8,128)S(1)}, u32[]{:S(2)}, u32[]{:S(2)}) collective-permute-start(f32[4,8,4096]{2,1,0:T(8,128)S(1)} %bitcast.80), channel_id=1, source_target_pairs={{0,2},{2,0},{4,6},{6,4},{8,10},{10,8},{12,14},{14,12},{16,18},{18,... | collective-permute-start | bytes 1572872 | tf_op jit(solution)/shard_map/ppermute | solution.py:42
  59.5 12.5 %collective-permute-done.4 = f32[4,8,4096]{2,1,0:T(8,128)S(1)} collective-permute-done((f32[4,8,4096]{2,1,0:T(8,128)S(1)}, f32[4,8,4096]{2,1,0:T(8,128)S(1)}, u32[]{:S(2)}, u32[]{:S(2)}) %collective-permute-start.4) | collective-permute-done | bytes 524320 | tf_op jit(solution)/shard_map/ppermute | solution.py:42
  73.1 2.1 %collective-permute-start.5 = (f32[4,4,4096]{2,0,1:T(4,128)S(1)}, f32[4,4,4096]{2,0,1:T(4,128)S(1)}, u32[]{:S(2)}, u32[]{:S(2)}) collective-permute-start(f32[4,4,4096]{2,0,1:T(4,128)S(1)} %dynamic-slice_bitcast_fusion), channel_id=1, source_target_pairs={{0,4},{4,0},{2,6},{6,2},{8,12},{12,8},{10,14},{14,10},{16,20},{20,... | collective-permute-start | bytes 786440 | tf_op jit(solution)/shard_map/ppermute | solution.py:42
  75.2 5.8 %collective-permute-done.5 = f32[4,4,4096]{2,0,1:T(4,128)S(1)} collective-permute-done((f32[4,4,4096]{2,0,1:T(4,128)S(1)}, f32[4,4,4096]{2,0,1:T(4,128)S(1)}, u32[]{:S(2)}, u32[]{:S(2)}) %collective-permute-start.5) | collective-permute-done | bytes 262176 | tf_op jit(solution)/shard_map/ppermute | solution.py:42
  81.9 4.5 %collective-permute-done.6 = f32[4,2,4096]{2,0,1:T(4,128)S(1)} collective-permute-done((f32[4,2,4096]{2,0,1:T(4,128)S(1)}, f32[4,2,4096]{2,0,1:T(4,128)S(1)}, u32[]{:S(2)}, u32[]{:S(2)}) %collective-permute-start.6) | collective-permute-done | bytes 131104 | tf_op jit(solution)/shard_map/ppermute | solution.py:42
  87.0 5.4 %collective-permute-done.7 = f32[4,1,4096]{2,0,1:T(4,128)S(1)} collective-permute-done((f32[4,1,4096]{2,0,1:T(4,128)S(1)}, f32[4,1,4096]{2,0,1:T(4,128)S(1)}, u32[]{:S(2)}, u32[]{:S(2)}) %collective-permute-start.7) | collective-permute-done | bytes 65568 | tf_op jit(solution)/shard_map/ppermute | solution.py:42
  92.5 0.7 add_bitcast_fusion
  (45 shorter events, 4.6 us)
Async XLA Ops:
  0.0 1.2 %copy-start = (f32[4,64,1024]{2,1,0:T(8,128)S(1)}, f32[4,64,1024]{2,1,0:T(8,128)}, u32[]{:S(2)}) copy-start(f32[4,64,1024]{2,1,0:T(8,128)} %param.7) | copy-start | bytes 3145732
  3.1 20.0 %collective-permute-start = (f32[2,64,1024]{2,1,0:T(8,128)}, f32[2,64,1024]{2,1,0:T(8,128)}, u32[]{:S(2)}, u32[]{:S(2)}) collective-permute-start(f32[2,64,1024]{2,1,0:T(8,128)} %get-tuple-element.78), channel_id=1, source_target_pairs={{0,2},{2,4},{4,6},{6,8},{8,10},{10,12},{12,14},{14,16},{16,18},{18... | collective-permute-start | bytes 1572872 | tf_op jit(solution)/shard_map/ppermute | solution.py:15
  6.5 24.7 %collective-permute-start.1 = (f32[2,64,1024]{2,1,0:T(8,128)}, f32[2,64,1024]{2,1,0:T(8,128)}, u32[]{:S(2)}, u32[]{:S(2)}) collective-permute-start(f32[2,64,1024]{2,1,0:T(8,128)} %get-tuple-element.79), channel_id=1, source_target_pairs={{2,0},{4,2},{6,4},{8,6},{10,8},{12,10},{14,12},{16,14},{18,16},{20... | collective-permute-start | bytes 1572872 | tf_op jit(solution)/shard_map/ppermute | solution.py:17
  12.6 2.9 %copy-start.3 = (f32[3,16]{1,0:T(4,128)S(1)}, f32[3,16]{1,0:T(4,128)}, u32[]{:S(2)}) copy-start(f32[3,16]{1,0:T(4,128)} %param.11) | copy-start | bytes 580
  12.6 2.9 %copy-start.4 = (f32[16]{0:T(128)S(1)}, f32[16]{0:T(128)}, u32[]{:S(2)}) copy-start(f32[16]{0:T(128)} %param.10) | copy-start | bytes 196
  32.2 2.6 %collective-permute-start.2 = (f32[8,2,1024]{2,1,0:T(2,128)S(1)}, f32[8,2,1024]{2,1,0:T(2,128)S(1)}, u32[]{:S(2)}, u32[]{:S(2)}) collective-permute-start(f32[8,2,1024]{2,1,0:T(2,128)S(1)} %get-tuple-element.58), channel_id=1, source_target_pairs={{0,1},{2,3},{4,5},{6,7},{8,9},{10,11},{12,13},{14,15},{16,17},{18,... | collective-permute-start | bytes 196616 | tf_op jit(solution)/shard_map/ppermute | solution.py:15
  33.5 3.1 %collective-permute-start.3 = (f32[8,2,1024]{2,1,0:T(2,128)S(1)}, f32[8,2,1024]{2,1,0:T(2,128)S(1)}, u32[]{:S(2)}, u32[]{:S(2)}) collective-permute-start(f32[8,2,1024]{2,1,0:T(2,128)S(1)} %get-tuple-element.59), channel_id=1, source_target_pairs={{1,0},{3,2},{5,4},{7,6},{9,8},{11,10},{13,12},{15,14},{17,16},{19,... | collective-permute-start | bytes 196616 | tf_op jit(solution)/shard_map/ppermute | solution.py:17
  44.6 1.0 %copy-start.2 = (f32[4,64,1024]{2,1,0:T(8,128)}, f32[4,64,1024]{2,1,0:T(8,128)S(1)}, u32[]{:S(2)}) copy-start(f32[4,64,1024]{2,1,0:T(8,128)S(1)} %get-tuple-element.55) | copy-start | bytes 3145732
  49.9 4.1 %copy-start.1 = (f32[4,4,64,1024]{3,2,1,0:T(8,128)S(1)}, f32[4,4,64,1024]{3,2,1,0:T(8,128)}, u32[]{:S(2)}) copy-start(f32[4,4,64,1024]{3,2,1,0:T(8,128)} %select_select_fusion) | copy-start | bytes 12582916
  57.9 14.1 %collective-permute-start.4 = (f32[4,8,4096]{2,1,0:T(8,128)S(1)}, f32[4,8,4096]{2,1,0:T(8,128)S(1)}, u32[]{:S(2)}, u32[]{:S(2)}) collective-permute-start(f32[4,8,4096]{2,1,0:T(8,128)S(1)} %bitcast.80), channel_id=1, source_target_pairs={{0,2},{2,0},{4,6},{6,4},{8,10},{10,8},{12,14},{14,12},{16,18},{18,... | collective-permute-start | bytes 1572872 | tf_op jit(solution)/shard_map/ppermute | solution.py:42
  73.1 7.9 %collective-permute-start.5 = (f32[4,4,4096]{2,0,1:T(4,128)S(1)}, f32[4,4,4096]{2,0,1:T(4,128)S(1)}, u32[]{:S(2)}, u32[]{:S(2)}) collective-permute-start(f32[4,4,4096]{2,0,1:T(4,128)S(1)} %dynamic-slice_bitcast_fusion), channel_id=1, source_target_pairs={{0,4},{4,0},{2,6},{6,2},{8,12},{12,8},{10,14},{14,10},{16,20},{20,... | collective-permute-start | bytes 786440 | tf_op jit(solution)/shard_map/ppermute | solution.py:42
  81.3 5.0 %collective-permute-start.6 = (f32[4,2,4096]{2,0,1:T(4,128)S(1)}, f32[4,2,4096]{2,0,1:T(4,128)S(1)}, u32[]{:S(2)}, u32[]{:S(2)}) collective-permute-start(f32[4,2,4096]{2,0,1:T(4,128)S(1)} %dynamic-slice_bitcast_fusion.1), channel_id=1, source_target_pairs={{0,8},{8,0},{2,10},{10,2},{4,12},{12,4},{6,14},{14,6},{16,24},{24,... | collective-permute-start | bytes 393224 | tf_op jit(solution)/shard_map/ppermute | solution.py:42
  86.6 5.8 %collective-permute-start.7 = (f32[4,1,4096]{2,0,1:T(4,128)S(1)}, f32[4,1,4096]{2,0,1:T(4,128)S(1)}, u32[]{:S(2)}, u32[]{:S(2)}) collective-permute-start(f32[4,1,4096]{2,0,1:T(4,128)S(1)} %constant_dynamic-slice_fusion), channel_id=1, source_target_pairs={{0,16},{16,0},{2,18},{18,2},{4,20},{20,4},{6,22},{22,6},{8,24},{24... | collective-permute-start | bytes 196616 | tf_op jit(solution)/shard_map/ppermute | solution.py:42
where the time goes:
time: 94.1 us; the launch traced here: 93.1 us
  waiting for transfers between devices  38.2 us (41%)
  other arithmetic  24.5 us (26%)
  starting transfers between devices  14.8 us (16%)
  local copies, waits for them, and re-layouts  9.18 us (10%)
  matrix products  4.12 us (4%)
  blocking collectives  1.83 us (2%)
    ppermute x4, waiting for transfers between devices, partner(): return lax.ppermute(block, axis, route)  28.3 us
    ppermute x2, waiting for transfers between devices, padded_2(): lax.ppermute(head, axis, [((i + 1) % count, i) for i in range(ends)])  9.87 us
    select_n x1, other arithmetic, material_props(): jnp.where(materials[None] == number, lookup_table[:, number][:, None, Non...  7.01 us
    ppermute x2, starting transfers between devices, padded_2(): lax.ppermute(head, axis, [((i + 1) % count, i) for i in range(ends)])  5.53 us
    ppermute x2, starting transfers between devices, padded_2(): lax.ppermute(tail, axis, [(i, (i + 1) % count) for i in range(ends)])  4.68 us
    ppermute x4, starting transfers between devices, partner(): return lax.ppermute(block, axis, route)  4.57 us
    dot_general x1, matrix products, shards(): jnp.einsum('zwy,wx->zxy', optical, earlier_cells, precision=lax.Precision...  4.12 us
    select_n x1, other arithmetic, shards(): second = jnp.where(keep_mask, smoothed, jnp.float32(0.0))  3.42 us
  transfers between devices with their start and end apart: 8, of which 6 were waited for; matrix products, arithmetic and copies ran while one was open for 13% of the time, Pallas kernels for 0%

commit v1 on v0

v1 whole, which is shorter than its diff:
```python
import functools

import jax
import jax.numpy as jnp
from jax import lax
from jax.experimental import pallas as pl
from jax.experimental.pallas import tpu as pltpu
from jax.sharding import PartitionSpec as P

SUB, LANE = 8, 128
VMEM_SPEC = pl.BlockSpec(memory_space=pltpu.VMEM)


def reorder_kernel(order_ref, density_ref, labels_ref, viewed_ref, materials_ref):
    rows = density_ref.shape[1]
    viewed_ref[0] = density_ref[0].reshape(rows, SUB, LANE)
    materials_ref[0] = labels_ref[0].reshape(rows, SUB, LANE)


def reorder(density, labels, order):
    slices, rows, columns = density.shape
    source = pl.BlockSpec((1, rows, columns), lambda i, o: (o[i], 0, 0))
    target = pl.BlockSpec((1, rows, SUB, LANE), lambda i, o: (i, 0, 0, 0))
    shape = (slices, rows, SUB, LANE)
    return pl.pallas_call(
        reorder_kernel,
        grid_spec=pltpu.PrefetchScalarGridSpec(
            num_scalar_prefetch=1,
            grid=(slices,),
            in_specs=[source, source],
            out_specs=[target, target],
        ),
        out_shape=[
            jax.ShapeDtypeStruct(shape, density.dtype),
            jax.ShapeDtypeStruct(shape, labels.dtype),
        ],
    )(order, density, labels)


def beside_y(cells, lane, first, last):
    low = pltpu.roll(cells, 1, 1)
    high = pltpu.roll(cells, LANE - 1, 1)
    low = jnp.where(lane == 0, pltpu.roll(low, 1, 0), low)
    high = jnp.where(lane == LANE - 1, pltpu.roll(high, SUB - 1, 0), high)
    return jnp.where(first, 0.0, low), jnp.where(last, 0.0, high)


def lookup(table, index):
    return jnp.take_along_axis(table, index, axis=1, mode="promise_in_bounds")


def shade_kernel(depth_count, light_count, wide, below, above, labels, tables, plain, lit, through, smooth):
    slices, rows = labels.shape[:2]
    depth_at = lax.axis_index("depth")
    light_at = lax.axis_index("light")
    lane = lax.broadcasted_iota(jnp.int32, (SUB, LANE), 1)
    sub = lax.broadcasted_iota(jnp.int32, (SUB, LANE), 0)
    first = (lane == 0) & (sub == 0)
    last = (lane == LANE - 1) & (sub == SUB - 1)
    has_below = (depth_at > 0).astype(jnp.float32)
    has_above = (depth_at < depth_count - 1).astype(jnp.float32)
    has_before = (light_at > 0).astype(jnp.float32)
    has_after = (light_at < light_count - 1).astype(jnp.float32)

    def cell(z, row):
        if z < 0:
            return below[z + 2, row]
        if z >= slices:
            return above[z - slices, row]
        return wide[z, row]

    def smooth_row(i, carry):
        column = [cell(z, i + 1) for z in range(-2, slices + 2)]
        for z in range(-1, slices + 1):
            center = column[z + 2]
            low, high = beside_y(center, lane, first, last)
            total = (column[z + 1] + column[z + 3]) + (cell(z, i) + cell(z, i + 2)) + (low + high)
            value = 0.4 * center + 0.1 * total
            if z < 0:
                value = value * has_below
            if z >= slices:
                value = value * has_above
            smooth[z + 1, i] = value
        return carry

    lax.fori_loop(0, rows + 2, smooth_row, 0)
    for z in range(slices):
        smooth[z + 1, 0] = smooth[z + 1, 0] * has_before
        smooth[z + 1, rows + 1] = smooth[z + 1, rows + 1] * has_after

    def shade_row(r, lights):
        lights = list(lights)
        remaining = jnp.ones((SUB, LANE), jnp.float32)
        flat = [jnp.zeros((SUB, LANE), jnp.float32) for _ in range(3)]
        for z in range(slices):
            center = smooth[z + 1, r + 1]
            low, high = beside_y(center, lane, first, last)
            grad_z = smooth[z + 2, r + 1] - smooth[z, r + 1]
            grad_x = smooth[z + 1, r + 2] - smooth[z + 1, r]
            grad_y = high - low
            facing = grad_x * lax.rsqrt(grad_z * grad_z + grad_x * grad_x + grad_y * grad_y + 0.2)
            index = labels[z, r]
            optical = lookup(tables[0], index) * jnp.exp(center)
            passed = jnp.exp(-optical)
            weight = (1.0 - passed) * remaining
            glow = weight * lights[z] * (0.5 + 0.5 * facing)
            faint = 0.2 * weight
            for c in range(3):
                albedo = lookup(tables[c + 1], index)
                flat[c] = flat[c] + albedo * faint
                lit[z * 3 + c, r] = albedo * glow
            remaining = remaining * passed
            lights[z] = lights[z] * passed
        for c in range(3):
            plain[c, r] = flat[c]
        plain[3, r] = 1.0 - remaining
        return tuple(lights)

    ones = tuple(jnp.ones((SUB, LANE), jnp.float32) for _ in range(slices))
    lights = lax.fori_loop(0, rows, shade_row, ones)
    for z in range(slices):
        through[z] = lights[z]


def shade(wide, below, above, labels, tables, depth_count, light_count):
    slices, rows = labels.shape[:2]
    f32 = jnp.float32
    return pl.pallas_call(
        functools.partial(shade_kernel, depth_count, light_count),
        in_specs=[VMEM_SPEC] * 5,
        out_specs=[VMEM_SPEC] * 3,
        out_shape=[
            jax.ShapeDtypeStruct((4, rows, SUB, LANE), f32),
            jax.ShapeDtypeStruct((slices * 3, rows, SUB, LANE), f32),
            jax.ShapeDtypeStruct((slices, SUB, LANE), f32),
        ],
        scratch_shapes=[pltpu.VMEM((slices + 2, rows + 2, SUB, LANE), f32)],
        compiler_params=pltpu.CompilerParams(vmem_limit_bytes=48 * 1024 * 1024),
    )(wide, below, above, labels, tables)


def both_ways(low_part, high_part, axis, count):
    from_low = lax.ppermute(high_part, axis, [(i, i + 1) for i in range(count - 1)])
    from_high = lax.ppermute(low_part, axis, [(i + 1, i) for i in range(count - 1)])
    return from_low, from_high


def partner(block, axis, stride):
    count = lax.axis_size(axis)
    route = []
    for low in range(count):
        high = low | 1 << stride
        if high != low and high < count:
            route += [(low, high), (high, low)]
    return lax.ppermute(block, axis, route)


def over_blend(front_part, back_part):
    return front_part + (1.0 - front_part[3:4]) * back_part


def shards(density, labels, slice_order, extinction, albedo):
    depth_count = lax.axis_size("depth")
    light_count = lax.axis_size("light")
    depth_at = lax.axis_index("depth")
    light_at = lax.axis_index("light")
    slices, rows, columns = density.shape
    viewed, materials = reorder(density, labels, slice_order % slices)
    before, after = both_ways(viewed[:, :2], viewed[:, -2:], "light", light_count)
    wide = jnp.concatenate([before, viewed, after], axis=1)
    below, above = both_ways(wide[:2], wide[-2:], "depth", depth_count)
    tables = jnp.concatenate([extinction[None, :], albedo], axis=0)
    tables = jnp.pad(tables, ((0, 0), (0, LANE - tables.shape[1])))
    tables = jnp.broadcast_to(tables[:, None, :], (4, SUB, LANE))
    plain, lit, through = shade(wide, below, above, materials, tables, depth_count, light_count)
    gathered = lax.all_gather(through, "light")
    incoming = jnp.ones_like(through)
    for k in range(light_count - 1):
        incoming = jnp.where(k < light_at, incoming * gathered[k], incoming)
    lit = lit.reshape(slices, 3, rows, SUB, LANE) * incoming[:, None, None]
    colour = plain[:3] + jnp.sum(lit, axis=0)
    current = jnp.concatenate([colour, plain[3:]], axis=0)
    current = current.reshape(4, depth_count, rows // depth_count if rows >= depth_count else 1, SUB, -1)
    for bit_number in range(depth_count.bit_length() - 1):
        blocks = current.shape[1]
        halves = current.reshape((4, blocks // 2, 2) + current.shape[2:])
        upper_bit = depth_at >> bit_number & 1
        kept_half = lax.dynamic_index_in_dim(halves, upper_bit, 2, False)
        given_half = lax.dynamic_index_in_dim(halves, 1 - upper_bit, 2, False)
        taken_half = partner(given_half, "depth", bit_number)
        in_front = jnp.where(upper_bit == 0, kept_half, taken_half)
        behind = jnp.where(upper_bit == 0, taken_half, kept_half)
        current = over_blend(in_front, behind)
    return current.reshape(4, -1)


def solution(mesh):
    return jax.shard_map(
        shards,
        mesh=mesh,
        in_specs=(P("depth", "light", None), P("depth", "light", None), P("depth"), P(), P()),
        out_specs=P(None, ("light", "depth")),
        check_vma=False,
    )
```

time: 94.1 us -> 96.8 us (1.029)
  other arithmetic: 24.5 us -> 4 us
  Pallas kernels: 0 us -> 19.3 us
  waiting for transfers between devices: 38.2 us -> 51.6 us
  local copies, waits for them, and re-layouts: 9.18 us -> 3.98 us
  matrix products: 4.12 us -> 0 us
    pallas_call x0 -> x2, Pallas kernels: none -> 19.3 us  [the longest x1 14.7 us: shade(): pl.pallas_call(functools.partial(shade_kernel, depth_count, light_count),...]
    ppermute x4, waiting for transfers between devices: 9.87 us -> 23 us  [the longest x2 11.5 us: both_ways(): lax.ppermute(high_part, axis, [(i, i + 1) for i in range(count - 1)])]
    select_n x3 -> x2, other arithmetic: 10.6 us -> 1.18 us  [the longest x1 1.17 us: shards(): viewed, materials = reorder(density, labels, slice_order % slices)]
    dot_general x1 -> x0, matrix products: 4.12 us -> none  [shards(): jnp.einsum('zwy,wx->zxy', optical, earlier_cells, precision=lax.Precision...]
    eq x1 -> x0, other arithmetic: 2.91 us -> none  [material_props(): materials[None] == number]
    gather x2 -> x0, local copies, waits for them, and re-layouts: 2.45 us -> none  [the longest x1 1.84 us: shards(): materials = jnp.take(labels, local_order, axis=0)]
    concatenate x2, other arithmetic: 2.2 us -> 0.08 us  [the longest x1 0.07 us: shards(): current = jnp.concatenate([colour, plain[3:]], axis=0)]
    another operation x1 -> x0, other arithmetic: 1.24 us -> none  [shards(): depth_total = jnp.cumsum(optical, axis=0)]
  transfers between devices with their start and end apart: 8 -> 8, of which waited for: 6 -> 7; matrix products, arithmetic and copies ran while one was open for 13% -> 1% of each run, Pallas kernels for 0% -> 0%
where the time goes in v1:
time: 96.8 us; the launch traced here: 95.5 us
  waiting for transfers between devices  51.6 us (53%)
  Pallas kernels  19.3 us (20%)
  starting transfers between devices  14.6 us (15%)
  other arithmetic  4 us (4%)
  local copies, waits for them, and re-layouts  3.98 us (4%)
  blocking collectives  1.82 us (2%)
    ppermute x4, waiting for transfers between devices, partner(): return lax.ppermute(block, axis, route)  28.6 us
    pallas_call x1, Pallas kernels, shade(): pl.pallas_call(functools.partial(shade_kernel, depth_count, light_count),...  14.7 us
    ppermute x2, waiting for transfers between devices, both_ways(): lax.ppermute(high_part, axis, [(i, i + 1) for i in range(count - 1)])  11.5 us
    ppermute x2, waiting for transfers between devices, both_ways(): lax.ppermute(low_part, axis, [(i + 1, i) for i in range(count - 1)])  11.5 us
    ppermute x2, starting transfers between devices, both_ways(): lax.ppermute(low_part, axis, [(i + 1, i) for i in range(count - 1)])  5.53 us
    ppermute x2, starting transfers between devices, both_ways(): lax.ppermute(high_part, axis, [(i, i + 1) for i in range(count - 1)])  5.12 us
    pallas_call x1, Pallas kernels, reorder(): pl.pallas_call(reorder_kernel, grid_spec=pltpu.PrefetchScalarGridSpec(num...  4.63 us
    ppermute x4, starting transfers between devices, partner(): return lax.ppermute(block, axis, route)  3.95 us
  transfers between devices with their start and end apart: 8, of which 7 were waited for; matrix products, arithmetic and copies ran while one was open for 1% of the time, Pallas kernels for 0%

profile of v1, /device:TPU:24, one launch (start us, length us, event | category | flops | bytes accessed | tf_op | source)
XLA Modules:
  0.0 95.5 jit_solution(1929932942586420914)
XLA Ops:
  0.0 1.2 %and_select_fusion.order_ref = s32[4]{0:T(128)} fusion(s32[4]{0:T(128)} %param.7), kind=kLoop, calls=%fused_computation.38 | loop fusion | flops 44 | bytes 32 | tf_op jit(solution)/shard_map/jit(remainder)/select_n | solution.py:168
  1.2 4.6 %shard_map.55 = (f32[4,64,8,128]{3,2,1,0:T(8,128)}, s32[4,64,8,128]{3,2,1,0:T(8,128)}) custom-call(s32[4]{0:T(128)} %and_select_fusion.order_ref, f32[4,64,1024]{2,1,0:T(8,128)} %density_ref.1, s32[4,64,1024]{2,1,0:T(8,128)} %labels_ref.1), custom_call_target="tpu_custom_call" | custom-call | tf_op jit(solution)/shard_map/pallas_call | solution.py:25
  5.8 0.8 fusion.12
  6.6 1.7 %collective-permute-start = (f32[4,2,8,128]{3,2,1,0:T(8,128)S(1)}, f32[4,2,8,128]{3,2,1,0:T(8,128)S(1)}, u32[]{:S(2)}, u32[]{:S(2)}) collective-permute-start(f32[4,2,8,128]{3,2,1,0:T(8,128)S(1)} %get-tuple-element.18), channel_id=1, source_target_pairs={{0,1},{2,3},{4,5},{6,7},{8,9},{10,11},{12,13},{14,15},{16,17},{18,... | collective-permute-start | bytes 98312 | tf_op jit(solution)/shard_map/ppermute | solution.py:143
  8.3 1.3 %collective-permute-start.1 = (f32[4,2,8,128]{3,2,1,0:T(8,128)S(1)}, f32[4,2,8,128]{3,2,1,0:T(8,128)S(1)}, u32[]{:S(2)}, u32[]{:S(2)}) collective-permute-start(f32[4,2,8,128]{3,2,1,0:T(8,128)S(1)} %get-tuple-element.17), channel_id=1, source_target_pairs={{1,0},{3,2},{5,4},{7,6},{9,8},{11,10},{13,12},{15,14},{17,16},{19,... | collective-permute-start | bytes 98312 | tf_op jit(solution)/shard_map/ppermute | solution.py:144
  9.6 0.0 collective-permute-done
  9.6 1.3 %constant_dynamic-update-slice_fusion.1 = f32[4,68,8,128]{3,2,1,0:T(8,128)S(1)} fusion(f32[4,68,8,128]{3,2,1,0:T(8,128)S(1)} %constant_dynamic-update-slice_fusion.2, f32[4,64,8,128]{3,2,1,0:T(8,128)} %get-tuple-element.10), kind=kLoop, calls=%fused_computation.31 | loop fusion | bytes 2097152
  10.9 0.5 collective-permute-done.1
  11.4 1.1 %fusion.11 = (f32[2,68,8,128]{3,2,1,0:T(8,128)}, f32[2,68,8,128]{3,2,1,0:T(8,128)}) fusion(f32[4,68,8,128]{3,2,1,0:T(8,128)S(1)} %constant_dynamic-update-slice_fusion.wide), kind=kLoop, calls=%fused_computation.40 | loop fusion | bytes 2228224 | tf_op jit(solution)/shard_map/slice | solution.py:171
  12.5 3.4 %collective-permute-start.2 = (f32[2,68,8,128]{3,2,1,0:T(8,128)}, f32[2,68,8,128]{3,2,1,0:T(8,128)S(1)}, u32[]{:S(2)}, u32[]{:S(2)}) collective-permute-start(f32[2,68,8,128]{3,2,1,0:T(8,128)} %get-tuple-element.16), channel_id=1, source_target_pairs={{0,2},{2,4},{4,6},{6,8},{8,10},{10,12},{12,14},{14,16},{16,18},{18... | collective-permute-start | bytes 1671176 | tf_op jit(solution)/shard_map/ppermute | solution.py:143
  15.9 4.2 %collective-permute-start.3 = (f32[2,68,8,128]{3,2,1,0:T(8,128)}, f32[2,68,8,128]{3,2,1,0:T(8,128)S(1)}, u32[]{:S(2)}, u32[]{:S(2)}) collective-permute-start(f32[2,68,8,128]{3,2,1,0:T(8,128)} %get-tuple-element.15), channel_id=1, source_target_pairs={{2,0},{4,2},{6,4},{8,6},{10,8},{12,10},{14,12},{16,14},{18,16},{20... | collective-permute-start | bytes 1671176 | tf_op jit(solution)/shard_map/ppermute | solution.py:144
  20.2 0.0 copy-done.1
  20.2 0.0 copy-done.2
  20.2 11.5 %collective-permute-done.2.below = f32[2,68,8,128]{3,2,1,0:T(8,128)S(1)} collective-permute-done((f32[2,68,8,128]{3,2,1,0:T(8,128)}, f32[2,68,8,128]{3,2,1,0:T(8,128)S(1)}, u32[]{:S(2)}, u32[]{:S(2)}) %collective-permute-start.2) | collective-permute-done | bytes 557088 | tf_op jit(solution)/shard_map/ppermute | solution.py:143
  31.7 11.0 %collective-permute-done.3.above = f32[2,68,8,128]{3,2,1,0:T(8,128)S(1)} collective-permute-done((f32[2,68,8,128]{3,2,1,0:T(8,128)}, f32[2,68,8,128]{3,2,1,0:T(8,128)S(1)}, u32[]{:S(2)}, u32[]{:S(2)}) %collective-permute-start.3) | collective-permute-done | bytes 557088 | tf_op jit(solution)/shard_map/ppermute | solution.py:144
  42.7 14.7 %shard_map.56 = (f32[4,64,8,128]{3,2,1,0:T(8,128)S(1)}, f32[12,64,8,128]{3,2,1,0:T(8,128)}, f32[4,8,128]{2,1,0:T(8,128)S(1)}) custom-call(f32[4,68,8,128]{3,2,1,0:T(8,128)S(1)} %constant_dynamic-update-slice_fusion.wide, f32[2,68,8,128]{3,2,1,0:T(8,128)S(1)} %collective-permute-done.2.below, f32[2,68,8,128]{3,2,1,0:T(8,128)S(1)} %collective-permute-done.3.above, ...), custom_call_target="tpu_custom_call" | custom-call | tf_op jit(solution)/shard_map/pallas_call | solution.py:128
  57.4 1.8 %all-gather = f32[8,8,128]{2,1,0:T(8,128)S(1)} all-gather(f32[4,8,128]{2,1,0:T(8,128)S(1)} %get-tuple-element.14), channel_id=2, replica_groups=mesh['depth'=16,'light'=2] {'light'}, dimensions={0}, use_global_device_ids=true | all-gather | bytes 49152 | tf_op jit(solution)/shard_map/all_gather | solution.py:176
  59.3 2.2 %multiply_reduce_fusion = f32[3,64,8,128]{3,2,1,0:T(8,128)S(1)} fusion(f32[4,3,64,8,128]{4,3,2,1,0:T(8,128)} %bitcast.58, f32[4,8,128]{2,1,0:T(8,128)S(1)} %slice_select_fusion), kind=kLoop, calls=%fused_computation | loop fusion | flops 1376256 | bytes 3948544 | tf_op jit(solution)/shard_map/reduce_sum | solution.py:181
  61.5 0.1 slice_add_fusion
  61.6 0.1 pad_maximum_fusion
  61.7 1.6 %collective-permute-start.4 = (f32[4,8,4,8,128]{4,3,2,1,0:T(8,128)S(1)}, f32[4,8,4,8,128]{4,3,2,1,0:T(8,128)S(1)}, u32[]{:S(2)}, u32[]{:S(2)}) collective-permute-start(f32[4,8,4,8,128]{4,3,2,1,0:T(8,128)S(1)} %dynamic-slice_bitcast_fusion), channel_id=1, source_target_pairs={{0,2},{2,0},{4,6},{6,4},{8,10},{10,8},{12,14},{14,12},{16,18},{18,... | collective-permute-start | bytes 1572872 | tf_op jit(solution)/shard_map/ppermute | solution.py:155
  63.3 12.5 %collective-permute-done.4 = f32[4,8,4,8,128]{4,3,2,1,0:T(8,128)S(1)} collective-permute-done((f32[4,8,4,8,128]{4,3,2,1,0:T(8,128)S(1)}, f32[4,8,4,8,128]{4,3,2,1,0:T(8,128)S(1)}, u32[]{:S(2)}, u32[]{:S(2)}) %collective-permute-start.4) | collective-permute-done | bytes 524320 | tf_op jit(solution)/shard_map/ppermute | solution.py:155
  75.8 0.1 bitcast_select_fusion.1
  75.9 0.1 fusion.1
  76.1 1.5 %collective-permute-start.5 = (f32[4,4,4,8,128]{4,3,2,1,0:T(8,128)S(1)}, f32[4,4,4,8,128]{4,3,2,1,0:T(8,128)S(1)}, u32[]{:S(2)}, u32[]{:S(2)}) collective-permute-start(f32[4,4,4,8,128]{4,3,2,1,0:T(8,128)S(1)} %dynamic-slice_bitcast_fusion.1), channel_id=1, source_target_pairs={{0,4},{4,0},{2,6},{6,2},{8,12},{12,8},{10,14},{14,10},{16,20},{20,... | collective-permute-start | bytes 786440 | tf_op jit(solution)/shard_map/ppermute | solution.py:155
  77.5 6.1 %collective-permute-done.5 = f32[4,4,4,8,128]{4,3,2,1,0:T(8,128)S(1)} collective-permute-done((f32[4,4,4,8,128]{4,3,2,1,0:T(8,128)S(1)}, f32[4,4,4,8,128]{4,3,2,1,0:T(8,128)S(1)}, u32[]{:S(2)}, u32[]{:S(2)}) %collective-permute-start.5) | collective-permute-done | bytes 262176 | tf_op jit(solution)/shard_map/ppermute | solution.py:155
  83.7 0.1 fusion.3
  83.8 0.5 collective-permute-start.6
  84.3 4.5 %collective-permute-done.6 = f32[4,2,4,8,128]{4,3,2,1,0:T(8,128)S(1)} collective-permute-done((f32[4,2,4,8,128]{4,3,2,1,0:T(8,128)S(1)}, f32[4,2,4,8,128]{4,3,2,1,0:T(8,128)S(1)}, u32[]{:S(2)}, u32[]{:S(2)}) %collective-permute-start.6) | collective-permute-done | bytes 131104 | tf_op jit(solution)/shard_map/ppermute | solution.py:155
  88.9 0.4 collective-permute-start.7
  89.3 5.5 %collective-permute-done.7 = f32[4,1,4,8,128]{4,3,2,1,0:T(8,128)S(1)} collective-permute-done((f32[4,1,4,8,128]{4,3,2,1,0:T(8,128)S(1)}, f32[4,1,4,8,128]{4,3,2,1,0:T(8,128)S(1)}, u32[]{:S(2)}, u32[]{:S(2)}) %collective-permute-start.7) | collective-permute-done | bytes 65568 | tf_op jit(solution)/shard_map/ppermute | solution.py:155
  94.9 0.7 copy.17
  (23 shorter events, 0.3 us)
Async XLA Ops:
  6.6 3.0 %collective-permute-start = (f32[4,2,8,128]{3,2,1,0:T(8,128)S(1)}, f32[4,2,8,128]{3,2,1,0:T(8,128)S(1)}, u32[]{:S(2)}, u32[]{:S(2)}) collective-permute-start(f32[4,2,8,128]{3,2,1,0:T(8,128)S(1)} %get-tuple-element.18), channel_id=1, source_target_pairs={{0,1},{2,3},{4,5},{6,7},{8,9},{10,11},{12,13},{14,15},{16,17},{18,... | collective-permute-start | bytes 98312 | tf_op jit(solution)/shard_map/ppermute | solution.py:143
  8.3 3.1 %collective-permute-start.1 = (f32[4,2,8,128]{3,2,1,0:T(8,128)S(1)}, f32[4,2,8,128]{3,2,1,0:T(8,128)S(1)}, u32[]{:S(2)}, u32[]{:S(2)}) collective-permute-start(f32[4,2,8,128]{3,2,1,0:T(8,128)S(1)} %get-tuple-element.17), channel_id=1, source_target_pairs={{1,0},{3,2},{5,4},{7,6},{9,8},{11,10},{13,12},{15,14},{17,16},{19,... | collective-permute-start | bytes 98312 | tf_op jit(solution)/shard_map/ppermute | solution.py:144
  11.4 8.8 %copy-start.1 = (f32[3,16]{1,0:T(4,128)S(1)}, f32[3,16]{1,0:T(4,128)}, u32[]{:S(2)}) copy-start(f32[3,16]{1,0:T(4,128)} %param.9) | copy-start | bytes 580
  11.4 8.8 %copy-start.2 = (f32[16]{0:T(128)S(1)}, f32[16]{0:T(128)}, u32[]{:S(2)}) copy-start(f32[16]{0:T(128)} %param.8) | copy-start | bytes 196
  11.4 31.3 %copy-start = (s32[4,64,8,128]{3,2,1,0:T(8,128)S(1)}, s32[4,64,8,128]{3,2,1,0:T(8,128)}, u32[]{:S(2)}) copy-start(s32[4,64,8,128]{3,2,1,0:T(8,128)} %get-tuple-element.11.labels) | copy-start | bytes 3145732
  12.5 19.2 %collective-permute-start.2 = (f32[2,68,8,128]{3,2,1,0:T(8,128)}, f32[2,68,8,128]{3,2,1,0:T(8,128)S(1)}, u32[]{:S(2)}, u32[]{:S(2)}) collective-permute-start(f32[2,68,8,128]{3,2,1,0:T(8,128)} %get-tuple-element.16), channel_id=1, source_target_pairs={{0,2},{2,4},{4,6},{6,8},{8,10},{10,12},{12,14},{14,16},{16,18},{18... | collective-permute-start | bytes 1671176 | tf_op jit(solution)/shard_map/ppermute | solution.py:143
  15.9 26.8 %collective-permute-start.3 = (f32[2,68,8,128]{3,2,1,0:T(8,128)}, f32[2,68,8,128]{3,2,1,0:T(8,128)S(1)}, u32[]{:S(2)}, u32[]{:S(2)}) collective-permute-start(f32[2,68,8,128]{3,2,1,0:T(8,128)} %get-tuple-element.15), channel_id=1, source_target_pairs={{2,0},{4,2},{6,4},{8,6},{10,8},{12,10},{14,12},{16,14},{18,16},{20... | collective-permute-start | bytes 1671176 | tf_op jit(solution)/shard_map/ppermute | solution.py:144
  61.7 14.1 %collective-permute-start.4 = (f32[4,8,4,8,128]{4,3,2,1,0:T(8,128)S(1)}, f32[4,8,4,8,128]{4,3,2,1,0:T(8,128)S(1)}, u32[]{:S(2)}, u32[]{:S(2)}) collective-permute-start(f32[4,8,4,8,128]{4,3,2,1,0:T(8,128)S(1)} %dynamic-slice_bitcast_fusion), channel_id=1, source_target_pairs={{0,2},{2,0},{4,6},{6,4},{8,10},{10,8},{12,14},{14,12},{16,18},{18,... | collective-permute-start | bytes 1572872 | tf_op jit(solution)/shard_map/ppermute | solution.py:155
  76.1 7.6 %collective-permute-start.5 = (f32[4,4,4,8,128]{4,3,2,1,0:T(8,128)S(1)}, f32[4,4,4,8,128]{4,3,2,1,0:T(8,128)S(1)}, u32[]{:S(2)}, u32[]{:S(2)}) collective-permute-start(f32[4,4,4,8,128]{4,3,2,1,0:T(8,128)S(1)} %dynamic-slice_bitcast_fusion.1), channel_id=1, source_target_pairs={{0,4},{4,0},{2,6},{6,2},{8,12},{12,8},{10,14},{14,10},{16,20},{20,... | collective-permute-start | bytes 786440 | tf_op jit(solution)/shard_map/ppermute | solution.py:155
  83.8 5.0 %collective-permute-start.6 = (f32[4,2,4,8,128]{4,3,2,1,0:T(8,128)S(1)}, f32[4,2,4,8,128]{4,3,2,1,0:T(8,128)S(1)}, u32[]{:S(2)}, u32[]{:S(2)}) collective-permute-start(f32[4,2,4,8,128]{4,3,2,1,0:T(8,128)S(1)} %dynamic-slice_bitcast_fusion.2), channel_id=1, source_target_pairs={{0,8},{8,0},{2,10},{10,2},{4,12},{12,4},{6,14},{14,6},{16,24},{24,... | collective-permute-start | bytes 393224 | tf_op jit(solution)/shard_map/ppermute | solution.py:155
  88.9 5.9 %collective-permute-start.7 = (f32[4,1,4,8,128]{4,3,2,1,0:T(8,128)S(1)}, f32[4,1,4,8,128]{4,3,2,1,0:T(8,128)S(1)}, u32[]{:S(2)}, u32[]{:S(2)}) collective-permute-start(f32[4,1,4,8,128]{4,3,2,1,0:T(8,128)S(1)} %constant_dynamic-slice_fusion), channel_id=1, source_target_pairs={{0,16},{16,0},{2,18},{18,2},{4,20},{20,4},{6,22},{22,6},{8,24},{24... | collective-permute-start | bytes 196616 | tf_op jit(solution)/shard_map/ppermute | solution.py:155

commit v2 on v1

--- a/solution.py
+++ b/solution.py
@@ -8,6 +8,7 @@
 from jax.sharding import PartitionSpec as P
 
 SUB, LANE = 8, 128
+MESH = pl.DeviceIdType.MESH
 VMEM_SPEC = pl.BlockSpec(memory_space=pltpu.VMEM)
 
 
@@ -49,25 +50,23 @@
     return jnp.take_along_axis(table, index, axis=1, mode="promise_in_bounds")
 
 
-def shade_kernel(depth_count, light_count, wide, below, above, labels, tables, plain, lit, through, smooth):
+def shade_kernel(depth_count, light_count, volume, labels, tables, plain, lit, through, smooth):
     slices, rows = labels.shape[:2]
     depth_at = lax.axis_index("depth")
     light_at = lax.axis_index("light")
+    pair_at = depth_at // 2
+    stripe_at = light_at * 2 + depth_at % 2
     lane = lax.broadcasted_iota(jnp.int32, (SUB, LANE), 1)
     sub = lax.broadcasted_iota(jnp.int32, (SUB, LANE), 0)
     first = (lane == 0) & (sub == 0)
     last = (lane == LANE - 1) & (sub == SUB - 1)
-    has_below = (depth_at > 0).astype(jnp.float32)
-    has_above = (depth_at < depth_count - 1).astype(jnp.float32)
-    has_before = (light_at > 0).astype(jnp.float32)
-    has_after = (light_at < light_count - 1).astype(jnp.float32)
+    has_below = (pair_at > 0).astype(jnp.float32)
+    has_above = (pair_at < depth_count // 2 - 1).astype(jnp.float32)
+    has_before = (stripe_at > 0).astype(jnp.float32)
+    has_after = (stripe_at < 2 * light_count - 1).astype(jnp.float32)
 
     def cell(z, row):
-        if z < 0:
-            return below[z + 2, row]
-        if z >= slices:
-            return above[z - slices, row]
-        return wide[z, row]
+        return volume[z + 2, row]
 
     def smooth_row(i, carry):
         column = [cell(z, i + 1) for z in range(-2, slices + 2)]
@@ -122,12 +121,12 @@
         through[z] = lights[z]
 
 
-def shade(wide, below, above, labels, tables, depth_count, light_count):
+def shade(volume, labels, tables, depth_count, light_count):
     slices, rows = labels.shape[:2]
     f32 = jnp.float32
     return pl.pallas_call(
         functools.partial(shade_kernel, depth_count, light_count),
-        in_specs=[VMEM_SPEC] * 5,
+        in_specs=[VMEM_SPEC] * 3,
         out_specs=[VMEM_SPEC] * 3,
         out_shape=[
             jax.ShapeDtypeStruct((4, rows, SUB, LANE), f32),
@@ -135,63 +134,468 @@
             jax.ShapeDtypeStruct((slices, SUB, LANE), f32),
         ],
         scratch_shapes=[pltpu.VMEM((slices + 2, rows + 2, SUB, LANE), f32)],
-        compiler_params=pltpu.CompilerParams(vmem_limit_bytes=48 * 1024 * 1024),
-    )(wide, below, above, labels, tables)
-
-
-def both_ways(low_part, high_part, axis, count):
-    from_low = lax.ppermute(high_part, axis, [(i, i + 1) for i in range(count - 1)])
-    from_high = lax.ppermute(low_part, axis, [(i + 1, i) for i in range(count - 1)])
-    return from_low, from_high
-
-
-def partner(block, axis, stride):
-    count = lax.axis_size(axis)
-    route = []
-    for low in range(count):
-        high = low | 1 << stride
-        if high != low and high < count:
-            route += [(low, high), (high, low)]
-    return lax.ppermute(block, axis, route)
-
-
-def over_blend(front_part, back_part):
-    return front_part + (1.0 - front_part[3:4]) * back_part
+        compiler_params=pltpu.CompilerParams(vmem_limit_bytes=40 * 1024 * 1024),
+    )(volume, labels, tables)
+
+
+def greet(wanted):
+    barrier = pltpu.get_barrier_semaphore()
+    count = 0
+    for exists, depth, light in wanted:
+
+        @pl.when(exists)
+        def _():
+            pl.semaphore_signal(barrier, inc=1, device_id=(depth, light), device_id_type=MESH)
+
+        count = count + jnp.where(exists, 1, 0)
+    pl.semaphore_wait(barrier, count)
+
+
+def trade_kernel(depth_count, light_count, viewed, materials, volume, labels, local_sem, send_sem, recv_sem):
+    slices, rows = viewed.shape[:2]
+    half = rows // 2
+    depth_at = lax.axis_index("depth")
+    light_at = lax.axis_index("light")
+    side = depth_at % 2
+    pair = depth_at // 2
+    even = pair * 2
+    other = even + 1 - side
+    has_below = pair > 0
+    has_above = pair < depth_count // 2 - 1
+    has_before = light_at > 0
+    has_after = light_at < light_count - 1
+    own = 2 + slices * side
+    wanted = [(depth_at >= 0, other, light_at)]
+    for exists, light in ((has_before, light_at - 1), (has_after, light_at + 1)):
+        wanted += [(exists, even, light), (exists, even + 1, light)]
+    wanted += [(has_below, depth_at - 2, light_at), (has_above, depth_at + 2, light_at)]
+
+    def piece(to_side):
+        return viewed.at[:, pl.ds((half - 2) * to_side, half + 2)]
+
+    def spot(from_side, to_side):
+        return volume.at[pl.ds(2 + slices * from_side, slices), pl.ds(2 - 2 * to_side, half + 2)]
+
+    keep = pltpu.make_async_copy(piece(side), spot(side, side), local_sem.at[0])
+    keep_labels = pltpu.make_async_copy(
+        materials.at[:, pl.ds(half * side, half)], labels.at[pl.ds(slices * side, slices)], local_sem.at[1]
+    )
+    keep.start()
+    keep_labels.start()
+    zeros2 = jnp.zeros((2, half + 4, SUB, LANE), jnp.float32)
+    zerosr = jnp.zeros((volume.shape[0] - 4, 2, SUB, LANE), jnp.float32)
+
+    @pl.when(jnp.logical_not(has_below))
+    def _():
+        volume[0:2] = zeros2
+
+    @pl.when(jnp.logical_not(has_above))
+    def _():
+        volume[2 * slices + 2 :] = zeros2
+
+    @pl.when(jnp.logical_not(has_before) & (side == 0))
+    def _():
+        volume[2 : 2 * slices + 2, 0:2] = zerosr
+
+    @pl.when(jnp.logical_not(has_after) & (side == 1))
+    def _():
+        volume[2 : 2 * slices + 2, half + 2 : half + 4] = zerosr
+
+    greet(wanted)
+
+    def remote(source, target, slot, depth, light):
+        return pltpu.make_async_remote_copy(
+            src_ref=source,
+            dst_ref=target,
+            send_sem=send_sem.at[slot],
+            recv_sem=recv_sem.at[slot],
+            device_id=(depth, light),
+            device_id_type=MESH,
+        )
+
+    swaps = []
+    for part in range(2):
+        two = slices // 2
+        swaps.append(
+            remote(
+                viewed.at[pl.ds(part * two, two), pl.ds((half - 2) * (1 - side), half + 2)],
+                volume.at[pl.ds(own + part * two, two), pl.ds(2 * side, half + 2)],
+                part,
+                other,
+                light_at,
+            )
+        )
+    swaps.append(
+        remote(
+            materials.at[:, pl.ds(half * (1 - side), half)], labels.at[pl.ds(slices * side, slices)], 2, other, light_at
+        )
+    )
+
+    def to_after(sender):
+        return volume.at[pl.ds(2 + slices * sender, slices), 0:2]
+
+    def to_before(sender):
+        return volume.at[pl.ds(2 + slices * sender, slices), half + 2 : half + 4]
+
+    def rim(source, target, slot, depth, light):
+        return pltpu.make_async_remote_copy(
+            src_ref=source,
+            dst_ref=target,
+            send_sem=send_sem.at[slot],
+            recv_sem=recv_sem.at[3 + side],
+            device_id=(depth, light),
+            device_id_type=MESH,
+        )
+
+    after_rim = rim(viewed.at[:, rows - 2 : rows], to_after(side), 3, even, light_at + 1)
+    before_rim = rim(viewed.at[:, 0:2], to_before(side), 4, even + 1, light_at - 1)
+
+    @pl.when(has_after)
+    def _():
+        after_rim.start()
+
+    @pl.when(has_before)
+    def _():
+        before_rim.start()
+
+    @pl.when(side == 0)
+    def _():
+        swaps[0].start()
+        swaps[1].start()
+
+    @pl.when(side == 1)
+    def _():
+        swaps[1].start()
+        swaps[0].start()
+
+    swaps[2].start()
+
+    def rim_wait(sender):
+        return pltpu.make_async_remote_copy(
+            src_ref=to_after(sender),
+            dst_ref=to_after(sender),
+            send_sem=send_sem.at[3],
+            recv_sem=recv_sem.at[3 + sender],
+            device_id=(other, light_at),
+            device_id_type=MESH,
+        )
+
+    @pl.when((has_before & (side == 0)) | (has_after & (side == 1)))
+    def _():
+        rim_wait(0).wait_recv()
+        rim_wait(1).wait_recv()
+
+    keep.wait()
+    below = remote(volume.at[2:4], volume.at[2 * slices + 2 : 2 * slices + 4], 5, depth_at - 2, light_at)
+    above = remote(volume.at[2 * slices : 2 * slices + 2], volume.at[0:2], 6, depth_at + 2, light_at)
+
+    @pl.when((side == 0) & has_below)
+    def _():
+        below.start()
+
+    @pl.when((side == 1) & has_above)
+    def _():
+        above.start()
+
+    @pl.when(side == 0)
+    def _():
+        swaps[1].wait_recv()
+
+    @pl.when(side == 1)
+    def _():
+        swaps[0].wait_recv()
+
+    @pl.when((side == 1) & has_below)
+    def _():
+        below.start()
+
+    @pl.when((side == 0) & has_above)
+    def _():
+        above.start()
+
+    @pl.when(side == 0)
+    def _():
+        swaps[0].wait_recv()
+
+    @pl.when(side == 1)
+    def _():
+        swaps[1].wait_recv()
+
+    swaps[2].wait_recv()
+    keep_labels.wait()
+
+    @pl.when(has_above)
+    def _():
+        below.wait_recv()
+
+    @pl.when(has_below)
+    def _():
+        above.wait_recv()
+
+    for one in swaps:
+        one.wait_send()
+
+    @pl.when(has_below)
+    def _():
+        below.wait_send()
+
+    @pl.when(has_above)
+    def _():
+        above.wait_send()
+
+    @pl.when(has_after)
+    def _():
+        after_rim.wait_send()
+
+    @pl.when(has_before)
+    def _():
+        before_rim.wait_send()
+
+
+def trade(viewed, materials, depth_count, light_count):
+    slices, rows = viewed.shape[:2]
+    half = rows // 2
+    return pl.pallas_call(
+        functools.partial(trade_kernel, depth_count, light_count),
+        in_specs=[VMEM_SPEC] * 2,
+        out_specs=[VMEM_SPEC] * 2,
+        out_shape=[
+            jax.ShapeDtypeStruct((2 * slices + 4, half + 4, SUB, LANE), jnp.float32),
+            jax.ShapeDtypeStruct((2 * slices, half, SUB, LANE), jnp.int32),
+        ],
+        scratch_shapes=[
+            pltpu.SemaphoreType.DMA((2,)),
+            pltpu.SemaphoreType.DMA((7,)),
+            pltpu.SemaphoreType.DMA((7,)),
+        ],
+        compiler_params=pltpu.CompilerParams(
+            collective_id=0, has_side_effects=True, vmem_limit_bytes=20 * 1024 * 1024
+        ),
+    )(viewed, materials)
+
+
+def over_blend(front, back):
+    through = 1.0 - front[3:4]
+    return front + through * back
+
+
+def merge_kernel(depth_count, light_count, plain, lit, through, image, blocks, *rest):
+    stages = depth_count.bit_length() - 3
+    taken = rest[:stages]
+    ends, shadow, send_sem, recv_sem, end_send, end_recv, shadow_send, shadow_recv = rest[stages:]
+    slices = through.shape[0]
+    block_rows = blocks.shape[2]
+    block_count = depth_count // 2
+    stripes = 2 * light_count
+    depth_at = lax.axis_index("depth")
+    light_at = lax.axis_index("light")
+    side = depth_at % 2
+    pair = depth_at // 2
+    stripe = light_at * 2 + side
+    top = pair // (block_count // 2)
+    low_bits = pair % (block_count // 2)
+
+    def flipped(b):
+        bit = (pair // (1 << b)) % 2
+        return bit, (pair + (1 - 2 * bit) * (1 << b)) * 2 + side
+
+    end_base = 2 * (side * (block_count // 2) + low_bits)
+    source0 = 2 * low_bits + top
+    source1 = 2 * (low_bits + block_count // 2) + top
+    wanted = [(k != stripe, pair * 2 + k % 2, k // 2) for k in range(stripes)]
+    wanted += [(depth_at >= 0, flipped(b)[1], light_at) for b in range(stages)]
+    for x in range(2):
+        wanted.append((end_base + x != depth_at, end_base + x, light_at))
+    ends_from = [(source0 != depth_at, source0), (source1 != depth_at, source1)]
+    wanted += [(exists, depth, light_at) for exists, depth in ends_from]
+    greet(wanted)
+
+    def shadow_copy(k, slot):
+        return pltpu.make_async_remote_copy(
+            src_ref=through,
+            dst_ref=shadow.at[slot],
+            send_sem=shadow_send.at[k],
+            recv_sem=shadow_recv.at[slot],
+            device_id=(pair * 2 + k % 2, k // 2),
+            device_id_type=MESH,
+        )
+
+    for k in range(1, stripes):
+
+        @pl.when(k > stripe)
+        def _():
+            shadow_copy(k, stripe).start()
+
+    for z in range(slices):
+        shadow[stripes, z] = jnp.ones((SUB, LANE), jnp.float32)
+    for k in range(stripes - 1):
+
+        @pl.when(k < stripe)
+        def _():
+            shadow_copy(k, k).wait_recv()
+            for z in range(slices):
+                shadow[stripes, z] = shadow[stripes, z] * shadow[k, z]
+
+    lights = [shadow[stripes, z] for z in range(slices)]
+
+    def finish(block):
+        def one_row(i, carry):
+            row = block * block_rows + i
+            for c in range(3):
+                value = plain[c, row]
+                for z in range(slices):
+                    value = value + lights[z] * lit[z * 3 + c, row]
+                blocks[block, c, i] = value
+            blocks[block, 3, i] = plain[3, row]
+            return carry
+
+        lax.fori_loop(0, block_rows, one_row, 0)
+
+    def index_of(b, n, bit):
+        x, upper = n % 2, n // 2
+        return x + 2 * ((pair % (1 << b)) + (bit + 2 * upper) * (1 << b))
+
+    def swap(b, n):
+        bit, depth = flipped(b)
+        slot = block_count - (block_count >> b) + n
+        return pltpu.make_async_remote_copy(
+            src_ref=blocks.at[index_of(b, n, 1 - bit)],
+            dst_ref=taken[b].at[n],
+            send_sem=send_sem.at[slot],
+            recv_sem=recv_sem.at[slot],
+            device_id=(depth, light_at),
+            device_id_type=MESH,
+        )
+
+    count0 = block_count // 2
+    bit0 = pair % 2
+    for n in range(count0):
+        finish(index_of(0, n, 1 - bit0))
+        swap(0, n).start()
+    for n in range(count0):
+        finish(index_of(0, n, bit0))
+
+    def blend_into(front_ref, back_ref, target_ref):
+        for i in range(block_rows):
+            clear = 1.0 - front_ref[3, i]
+            for c in range(4):
+                target_ref[c, i] = front_ref[c, i] + clear * back_ref[c, i]
+
+    def blend(b, n):
+        bit, depth = flipped(b)
+        swap(b, n).wait_recv()
+        mine = blocks.at[index_of(b, n, bit)]
+
+        @pl.when(bit == 0)
+        def _():
+            blend_into(mine, taken[b].at[n], mine)
+
+        @pl.when(bit == 1)
+        def _():
+            blend_into(taken[b].at[n], mine, mine)
+
+    def end_copy(x, slot):
+        return pltpu.make_async_remote_copy(
+            src_ref=blocks.at[x + 2 * low_bits],
+            dst_ref=ends.at[slot],
+            send_sem=end_send.at[x],
+            recv_sem=end_recv.at[slot],
+            device_id=(end_base + x, light_at),
+            device_id_type=MESH,
+        )
+
+    for b in range(stages):
+        count = block_count >> (b + 1)
+        bit, depth = flipped(b)
+        if b + 1 < stages:
+            for n in range(count):
+                blend(b, n)
+            for n in range(count // 2):
+                swap(b + 1, n).start()
+        else:
+            for n in range(count):
+                blend(b, n)
+    for x in range(2):
+
+        @pl.when(end_base + x != depth_at)
+        def _():
+            end_copy(x, top).start()
+
+    stay = source0 == depth_at
+    stay_late = source1 == depth_at
+    mine = blocks.at[side + 2 * low_bits]
+
+    @pl.when(jnp.logical_not(stay))
+    def _():
+        end_copy(0, 0).wait_recv()
+
+    @pl.when(jnp.logical_not(stay_late))
+    def _():
+        end_copy(0, 1).wait_recv()
+
+    @pl.when(stay)
+    def _():
+        blend_into(mine, ends.at[1], image)
+
+    @pl.when(stay_late)
+    def _():
+        blend_into(ends.at[0], mine, image)
+
+    @pl.when(jnp.logical_not(stay | stay_late))
+    def _():
+        blend_into(ends.at[0], ends.at[1], image)
+
+    for b in range(stages):
+        for n in range(block_count >> (b + 1)):
+            swap(b, n).wait_send()
+    for x in range(2):
+
+        @pl.when(end_base + x != depth_at)
+        def _():
+            end_copy(x, top).wait_send()
+
+    for k in range(1, stripes):
+
+        @pl.when(k > stripe)
+        def _():
+            shadow_copy(k, stripe).wait_send()
+
+
+def merge(plain, lit, through, depth_count, light_count):
+    rows, slices = plain.shape[1], through.shape[0]
+    f32 = jnp.float32
+    block_count = depth_count // 2
+    block = (4, rows // block_count, SUB, LANE)
+    stages = depth_count.bit_length() - 3
+    stripes = 2 * light_count
+    dma = pltpu.SemaphoreType.DMA
+    scratch = [pltpu.VMEM((block_count,) + block, f32)]
+    scratch += [pltpu.VMEM((block_count >> (b + 1),) + block, f32) for b in range(stages)]
+    scratch += [pltpu.VMEM((2,) + block, f32), pltpu.VMEM((stripes + 1, slices, SUB, LANE), f32)]
+    scratch += [dma((block_count,)), dma((block_count,)), dma((2,)), dma((2,)), dma((stripes,)), dma((stripes,))]
+    return pl.pallas_call(
+        functools.partial(merge_kernel, depth_count, light_count),
+        in_specs=[VMEM_SPEC] * 3,
+        out_specs=VMEM_SPEC,
+        out_shape=jax.ShapeDtypeStruct(block, f32),
+        scratch_shapes=scratch,
+        compiler_params=pltpu.CompilerParams(
+            collective_id=1, has_side_effects=True, vmem_limit_bytes=40 * 1024 * 1024
+        ),
+    )(plain, lit, through)
 
 
 def shards(density, labels, slice_order, extinction, albedo):
     depth_count = lax.axis_size("depth")
     light_count = lax.axis_size("light")
-    depth_at = lax.axis_index("depth")
-    light_at = lax.axis_index("light")
     slices, rows, columns = density.shape
     viewed, materials = reorder(density, labels, slice_order % slices)
-    before, after = both_ways(viewed[:, :2], viewed[:, -2:], "light", light_count)
-    wide = jnp.concatenate([before, viewed, after], axis=1)
-    below, above = both_ways(wide[:2], wide[-2:], "depth", depth_count)
+    volume, stripe_labels = trade(viewed, materials, depth_count, light_count)
     tables = jnp.concatenate([extinction[None, :], albedo], axis=0)
     tables = jnp.pad(tables, ((0, 0), (0, LANE - tables.shape[1])))
     tables = jnp.broadcast_to(tables[:, None, :], (4, SUB, LANE))
-    plain, lit, through = shade(wide, below, above, materials, tables, depth_count, light_count)
-    gathered = lax.all_gather(through, "light")
-    incoming = jnp.ones_like(through)
-    for k in range(light_count - 1):
-        incoming = jnp.where(k < light_at, incoming * gathered[k], incoming)
-    lit = lit.reshape(slices, 3, rows, SUB, LANE) * incoming[:, None, None]
-    colour = plain[:3] + jnp.sum(lit, axis=0)
-    current = jnp.concatenate([colour, plain[3:]], axis=0)
-    current = current.reshape(4, depth_count, rows // depth_count if rows >= depth_count else 1, SUB, -1)
-    for bit_number in range(depth_count.bit_length() - 1):
-        blocks = current.shape[1]
-        halves = current.reshape((4, blocks // 2, 2) + current.shape[2:])
-        upper_bit = depth_at >> bit_number & 1
-        kept_half = lax.dynamic_index_in_dim(halves, upper_bit, 2, False)
-        given_half = lax.dynamic_index_in_dim(halves, 1 - upper_bit, 2, False)
-        taken_half = partner(given_half, "depth", bit_number)
-        in_front = jnp.where(upper_bit == 0, kept_half, taken_half)
-        behind = jnp.where(upper_bit == 0, taken_half, kept_half)
-        current = over_blend(in_front, behind)
-    return current.reshape(4, -1)
+    plain, lit, through = shade(volume, stripe_labels, tables, depth_count, light_count)
+    return merge(plain, lit, through, depth_count, light_count).reshape(4, -1)
 
 
 def solution(mesh):

time: 96.8 us -> 68.9 us (0.71); the launches traced: 95.5 us -> 68.6 us
  waiting for transfers between devices: 51.6 us -> 0 us
  Pallas kernels: 19.3 us -> 63.6 us
  starting transfers between devices: 14.6 us -> 0 us
  other arithmetic: 4 us -> 1.86 us
  blocking collectives: 1.82 us -> 0 us
    ppermute x8 -> x0, waiting for transfers between devices: 51.6 us -> none  [the longest x4 28.6 us: partner(): return lax.ppermute(block, axis, route)]
    pallas_call x0 -> x2, Pallas kernels: none -> 50.6 us  [the longest x1 27.2 us: trade(): pl.pallas_call(functools.partial(trade_kernel, depth_count, light_count),...]
    ppermute x8 -> x0, starting transfers between devices: 14.6 us -> none  [the longest x2 5.53 us: both_ways(): lax.ppermute(low_part, axis, [(i + 1, i) for i in range(count - 1)])]
    pallas_call x1, Pallas kernels: 14.7 us -> 8.38 us  [shade(): pl.pallas_call(functools.partial(shade_kernel, depth_count, light_count),...]
    reduce_sum x1 -> x0, other arithmetic: 2.23 us -> none  [shards(): colour = plain[:3] + jnp.sum(lit, axis=0)]
    slice x3 -> x0, local copies, waits for them, and re-layouts: 1.88 us -> none  [the longest x1 1.09 us: shards(): below, above = both_ways(wide[:2], wide[-2:], 'depth', depth_count)]
    all_gather x1 -> x0, blocking collectives: 1.82 us -> none  [shards(): gathered = lax.all_gather(through, 'light')]
    unnamed x9 -> x5, local copies, waits for them, and re-layouts: 1.98 us -> 3.12 us
  transfers between devices with their start and end apart: 8 -> 0, of which waited for: 7 -> 0; matrix products, arithmetic and copies ran while one was open for 1% -> 0% of each run, Pallas kernels for 0% -> 0%
where the time goes in v2:
time: 68.9 us; the launch traced here: 68.6 us
  Pallas kernels  63.6 us (92%)
  local copies, waits for them, and re-layouts  3.13 us (5%)
  other arithmetic  1.86 us (3%)
    pallas_call x1, Pallas kernels, trade(): pl.pallas_call(functools.partial(trade_kernel, depth_count, light_count),...  27.2 us
    pallas_call x1, Pallas kernels, merge(): pl.pallas_call(functools.partial(merge_kernel, depth_count, light_count),...  23.4 us
    pallas_call x1, Pallas kernels, shade(): pl.pallas_call(functools.partial(shade_kernel, depth_count, light_count),...  8.38 us
    pallas_call x1, Pallas kernels, reorder(): pl.pallas_call(reorder_kernel, grid_spec=pltpu.PrefetchScalarGridSpec(num...  4.61 us
    unnamed x5, local copies, waits for them, and re-layouts  3.12 us

profile of v2, /device:TPU:24, one launch (start us, length us, event | category | flops | bytes accessed | tf_op | source)
XLA Modules:
  0.0 68.6 jit_solution(2025121672521858137)
XLA Ops:
  0.0 1.2 %and_select_fusion.order_ref = s32[4]{0:T(128)} fusion(s32[4]{0:T(128)} %param.7), kind=kLoop, calls=%fused_computation.5 | loop fusion | flops 44 | bytes 32 | tf_op jit(solution)/shard_map/jit(remainder)/select_n | solution.py:592
  1.2 0.7 %select_maximum_fusion = f32[4,128]{1,0:T(4,128)S(1)} fusion(f32[3,16]{1,0:T(4,128)} %param.9, f32[1,16]{1,0:T(1,128)} %bitcast.7), kind=kLoop, calls=%fused_computation.3 | loop fusion | flops 2048 | bytes 2304 | tf_op jit(solution)/shard_map/concatenate | solution.py:594
  1.9 4.6 %shard_map.55 = (f32[4,64,8,128]{3,2,1,0:T(8,128)}, s32[4,64,8,128]{3,2,1,0:T(8,128)}) custom-call(s32[4]{0:T(128)} %and_select_fusion.order_ref, f32[4,64,1024]{2,1,0:T(8,128)} %density_ref.1, s32[4,64,1024]{2,1,0:T(8,128)} %labels_ref.1), custom_call_target="tpu_custom_call" | custom-call | tf_op jit(solution)/shard_map/pallas_call | solution.py:26
  6.5 0.0 copy-start
  6.5 1.2 %copy-done = f32[4,64,8,128]{3,2,1,0:T(8,128)S(1)} copy-done((f32[4,64,8,128]{3,2,1,0:T(8,128)S(1)}, f32[4,64,8,128]{3,2,1,0:T(8,128)}, u32[]{:S(2)}) %copy-start) | copy-done | bytes 1048600
  7.7 0.0 copy-start.1
  7.7 1.2 %copy-done.1 = s32[4,64,8,128]{3,2,1,0:T(8,128)S(1)} copy-done((s32[4,64,8,128]{3,2,1,0:T(8,128)S(1)}, s32[4,64,8,128]{3,2,1,0:T(8,128)}, u32[]{:S(2)}) %copy-start.1) | copy-done | bytes 1048600
  8.9 27.2 %shard_map.56 = (f32[12,36,8,128]{3,2,1,0:T(8,128)S(1)}, s32[8,32,8,128]{3,2,1,0:T(8,128)S(1)}) custom-call(f32[4,64,8,128]{3,2,1,0:T(8,128)S(1)} %copy-done, s32[4,64,8,128]{3,2,1,0:T(8,128)S(1)} %copy-done.1), custom_call_target="tpu_custom_call" | custom-call | tf_op jit(solution)/shard_map/pallas_call | solution.py:358
  36.2 8.4 %shard_map.57 = (f32[4,32,8,128]{3,2,1,0:T(8,128)S(1)}, f32[24,32,8,128]{3,2,1,0:T(8,128)S(1)}, f32[8,8,128]{2,1,0:T(8,128)S(1)}) custom-call(f32[12,36,8,128]{3,2,1,0:T(8,128)S(1)} %get-tuple-element.14.volume, s32[8,32,8,128]{3,2,1,0:T(8,128)S(1)} %get-tuple-element.15.labels, f32[4,8,128]{2,1,0:T(8,128)S(1)} %broadcast_in_dim.10.tables), custom_call_target="tpu_custom_call" | custom-call | tf_op jit(solution)/shard_map/pallas_call | solution.py:127
  44.6 23.4 %shard_map.58 = f32[4,4,8,128]{3,2,1,0:T(8,128)S(1)} custom-call(f32[4,32,8,128]{3,2,1,0:T(8,128)S(1)} %get-tuple-element.16.plain, f32[24,32,8,128]{3,2,1,0:T(8,128)S(1)} %get-tuple-element.17.lit, f32[8,8,128]{2,1,0:T(8,128)S(1)} %get-tuple-element.18.through), custom_call_target="tpu_custom_call" | custom-call | tf_op jit(solution)/shard_map/pallas_call | solution.py:576
  68.0 0.7 copy.8
  (1 shorter events, 0.0 us)
Async XLA Ops:
  6.5 1.2 %copy-start = (f32[4,64,8,128]{3,2,1,0:T(8,128)S(1)}, f32[4,64,8,128]{3,2,1,0:T(8,128)}, u32[]{:S(2)}) copy-start(f32[4,64,8,128]{3,2,1,0:T(8,128)} %get-tuple-element.12.viewed) | copy-start | bytes 3145732
  7.7 1.2 %copy-start.1 = (s32[4,64,8,128]{3,2,1,0:T(8,128)S(1)}, s32[4,64,8,128]{3,2,1,0:T(8,128)}, u32[]{:S(2)}) copy-start(s32[4,64,8,128]{3,2,1,0:T(8,128)} %get-tuple-element.13.materials) | copy-start | bytes 3145732

commit v3 on v2

--- a/solution.py
+++ b/solution.py
@@ -12,29 +12,41 @@
 VMEM_SPEC = pl.BlockSpec(memory_space=pltpu.VMEM)
 
 
-def reorder_kernel(order_ref, density_ref, labels_ref, viewed_ref, materials_ref):
-    rows = density_ref.shape[1]
-    viewed_ref[0] = density_ref[0].reshape(rows, SUB, LANE)
-    materials_ref[0] = labels_ref[0].reshape(rows, SUB, LANE)
+def reorder_kernel(order, density, labels, viewed, materials, held, held_labels, sems):
+    slices, rows = density.shape[:2]
+    copies = []
+    for source, target, base in ((density, held, 0), (labels, held_labels, slices)):
+        for z in range(slices):
+            at = lax.rem(order[z], slices)
+            copies.append(pltpu.make_async_copy(source.at[at], target.at[z], sems.at[base + z]))
+    for one in copies:
+        one.start()
+    for z in range(slices):
+        copies[z].wait()
+        viewed[z] = held[z].reshape(rows, SUB, LANE)
+    for z in range(slices):
+        copies[slices + z].wait()
+        materials[z] = held_labels[z].reshape(rows, SUB, LANE)
 
 
 def reorder(density, labels, order):
     slices, rows, columns = density.shape
-    source = pl.BlockSpec((1, rows, columns), lambda i, o: (o[i], 0, 0))
-    target = pl.BlockSpec((1, rows, SUB, LANE), lambda i, o: (i, 0, 0, 0))
     shape = (slices, rows, SUB, LANE)
+    far = pl.BlockSpec(memory_space=pltpu.HBM)
     return pl.pallas_call(
         reorder_kernel,
-        grid_spec=pltpu.PrefetchScalarGridSpec(
-            num_scalar_prefetch=1,
-            grid=(slices,),
-            in_specs=[source, source],
-            out_specs=[target, target],
-        ),
+        in_specs=[pl.BlockSpec(memory_space=pltpu.SMEM), far, far],
+        out_specs=[VMEM_SPEC] * 2,
         out_shape=[
             jax.ShapeDtypeStruct(shape, density.dtype),
             jax.ShapeDtypeStruct(shape, labels.dtype),
         ],
+        scratch_shapes=[
+            pltpu.VMEM(density.shape, density.dtype),
+            pltpu.VMEM(labels.shape, labels.dtype),
+            pltpu.SemaphoreType.DMA((2 * slices,)),
+        ],
+        compiler_params=pltpu.CompilerParams(vmem_limit_bytes=12 * 1024 * 1024),
     )(order, density, labels)
 
 
@@ -50,7 +62,7 @@
     return jnp.take_along_axis(table, index, axis=1, mode="promise_in_bounds")
 
 
-def shade_kernel(depth_count, light_count, volume, labels, tables, plain, lit, through, smooth):
+def shade_kernel(depth_count, light_count, volume, labels, extinction, albedo, plain, lit, through, smooth):
     slices, rows = labels.shape[:2]
     depth_at = lax.axis_index("depth")
     light_at = lax.axis_index("light")
@@ -60,6 +72,11 @@
     sub = lax.broadcasted_iota(jnp.int32, (SUB, LANE), 0)
     first = (lane == 0) & (sub == 0)
     last = (lane == LANE - 1) & (sub == SUB - 1)
+    tables = [jnp.zeros((SUB, LANE), jnp.float32) for _ in range(4)]
+    for k in range(extinction.shape[0]):
+        tables[0] = jnp.where(lane == k, extinction[k], tables[0])
+        for c in range(3):
+            tables[c + 1] = jnp.where(lane == k, albedo[c, k], tables[c + 1])
     has_below = (pair_at > 0).astype(jnp.float32)
     has_above = (pair_at < depth_count // 2 - 1).astype(jnp.float32)
     has_before = (stripe_at > 0).astype(jnp.float32)
@@ -105,9 +122,9 @@
             glow = weight * lights[z] * (0.5 + 0.5 * facing)
             faint = 0.2 * weight
             for c in range(3):
-                albedo = lookup(tables[c + 1], index)
-                flat[c] = flat[c] + albedo * faint
-                lit[z * 3 + c, r] = albedo * glow
+                tint = lookup(tables[c + 1], index)
+                flat[c] = flat[c] + tint * faint
+                lit[z * 3 + c, r] = tint * glow
             remaining = remaining * passed
             lights[z] = lights[z] * passed
         for c in range(3):
@@ -121,12 +138,12 @@
         through[z] = lights[z]
 
 
-def shade(volume, labels, tables, depth_count, light_count):
+def shade(volume, labels, extinction, albedo, depth_count, light_count):
     slices, rows = labels.shape[:2]
     f32 = jnp.float32
     return pl.pallas_call(
         functools.partial(shade_kernel, depth_count, light_count),
-        in_specs=[VMEM_SPEC] * 3,
+        in_specs=[VMEM_SPEC] * 2 + [pl.BlockSpec(memory_space=pltpu.SMEM)] * 2,
         out_specs=[VMEM_SPEC] * 3,
         out_shape=[
             jax.ShapeDtypeStruct((4, rows, SUB, LANE), f32),
@@ -135,7 +152,7 @@
         ],
         scratch_shapes=[pltpu.VMEM((slices + 2, rows + 2, SUB, LANE), f32)],
         compiler_params=pltpu.CompilerParams(vmem_limit_bytes=40 * 1024 * 1024),
-    )(volume, labels, tables)
+    )(volume, labels, extinction, albedo)
 
 
 def greet(wanted):
@@ -452,7 +469,13 @@
         lax.fori_loop(0, block_rows, one_row, 0)
 
     def index_of(b, n, bit):
+        uppers = block_count >> (b + 2)
         x, upper = n % 2, n // 2
+        if uppers >= 2:
+            later = (pair // (1 << (b + 1))) % 2
+            rest = n % uppers
+            x = rest % 2
+            upper = 2 * (rest // 2) + (1 - later if n < uppers else later)
         return x + 2 * ((pair % (1 << b)) + (bit + 2 * upper) * (1 << b))
 
     def swap(b, n):
@@ -508,18 +531,19 @@
         count = block_count >> (b + 1)
         bit, depth = flipped(b)
         if b + 1 < stages:
-            for n in range(count):
+            for n in range(count // 2):
                 blend(b, n)
             for n in range(count // 2):
                 swap(b + 1, n).start()
+            for n in range(count // 2, count):
+                blend(b, n)
         else:
-            for n in range(count):
-                blend(b, n)
-    for x in range(2):
-
-        @pl.when(end_base + x != depth_at)
-        def _():
-            end_copy(x, top).start()
+            for x in range(2):
+                blend(b, x)
+
+                @pl.when(end_base + x != depth_at)
+                def _():
+                    end_copy(x, top).start()
 
     stay = source0 == depth_at
     stay_late = source1 == depth_at
@@ -589,12 +613,9 @@
     depth_count = lax.axis_size("depth")
     light_count = lax.axis_size("light")
     slices, rows, columns = density.shape
-    viewed, materials = reorder(density, labels, slice_order % slices)
+    viewed, materials = reorder(density, labels, slice_order)
     volume, stripe_labels = trade(viewed, materials, depth_count, light_count)
-    tables = jnp.concatenate([extinction[None, :], albedo], axis=0)
-    tables = jnp.pad(tables, ((0, 0), (0, LANE - tables.shape[1])))
-    tables = jnp.broadcast_to(tables[:, None, :], (4, SUB, LANE))
-    plain, lit, through = shade(volume, stripe_labels, tables, depth_count, light_count)
+    plain, lit, through = shade(volume, stripe_labels, extinction, albedo, depth_count, light_count)
     return merge(plain, lit, through, depth_count, light_count).reshape(4, -1)
 
 

time: 68.9 us -> 61.2 us (0.89)
  Pallas kernels: 63.6 us -> 57.2 us
  other arithmetic: 1.86 us -> 0 us
    pallas_call x1, Pallas kernels: 23.4 us -> 19.7 us  [merge(): pl.pallas_call(functools.partial(merge_kernel, depth_count, light_count),...]
    pallas_call x1, Pallas kernels: 4.61 us -> 1.25 us  [reorder(): pl.pallas_call(reorder_kernel, in_specs=[pl.BlockSpec(memory_space=pltpu....]
    select_n x1 -> x0, other arithmetic: 1.17 us -> none  [shards(): viewed, materials = reorder(density, labels, slice_order % slices)]
    concatenate x1 -> x0, other arithmetic: 0.69 us -> none  [shards(): tables = jnp.concatenate([extinction[None, :], albedo], axis=0)]
    unnamed x5 -> x11, local copies, waits for them, and re-layouts: 3.12 us -> 3.78 us
where the time goes in v3:
time: 61.2 us; the launch traced here: 61 us
  Pallas kernels  57.2 us (93%)
  local copies, waits for them, and re-layouts  3.78 us (6%)
    pallas_call x1, Pallas kernels, trade(): pl.pallas_call(functools.partial(trade_kernel, depth_count, light_count),...  27.3 us
    pallas_call x1, Pallas kernels, merge(): pl.pallas_call(functools.partial(merge_kernel, depth_count, light_count),...  19.7 us
    pallas_call x1, Pallas kernels, shade(): pl.pallas_call(functools.partial(shade_kernel, depth_count, light_count),...  8.93 us
    unnamed x11, local copies, waits for them, and re-layouts  3.78 us
    pallas_call x1, Pallas kernels, reorder(): pl.pallas_call(reorder_kernel, in_specs=[pl.BlockSpec(memory_space=pltpu....  1.25 us

profile of v3, /device:TPU:24, one launch (start us, length us, event | category | flops | bytes accessed | tf_op | source)
XLA Modules:
  0.0 61.0 jit_solution(1792515780016753088)
XLA Ops:
  0.0 0.0 copy-start
  0.0 1.2 %copy-done = f32[4,64,1024]{2,1,0:T(8,128)S(1)} copy-done((f32[4,64,1024]{2,1,0:T(8,128)S(1)}, f32[4,64,1024]{2,1,0:T(8,128)}, u32[]{:S(2)}) %copy-start) | copy-done | bytes 1048600
  1.2 0.0 copy-start.1
  1.2 1.2 %copy-done.1 = s32[4,64,1024]{2,1,0:T(8,128)S(1)} copy-done((s32[4,64,1024]{2,1,0:T(8,128)S(1)}, s32[4,64,1024]{2,1,0:T(8,128)}, u32[]{:S(2)}) %copy-start.1) | copy-done | bytes 1048600
  2.5 0.0 copy-start.3
  2.5 0.7 %copy-done.3 = s32[4]{0:T(128)S(1)} copy-done((s32[4]{0:T(128)S(1)}, s32[4]{0:T(128)}, u32[]{:S(2)}) %copy-start.3) | copy-done | bytes 40
  3.1 0.0 copy-start.2
  3.1 0.0 copy-start.4
  3.1 1.3 %shard_map.55 = (f32[4,64,8,128]{3,2,1,0:T(8,128)S(1)}, s32[4,64,8,128]{3,2,1,0:T(8,128)S(1)}) custom-call(s32[4]{0:T(128)S(1)} %copy-done.3, f32[4,64,1024]{2,1,0:T(8,128)S(1)} %copy-done, s32[4,64,1024]{2,1,0:T(8,128)S(1)} %copy-done.1), custom_call_target="tpu_custom_call" | custom-call | tf_op jit(solution)/shard_map/pallas_call | solution.py:36
  4.4 27.3 %shard_map.56 = (f32[12,36,8,128]{3,2,1,0:T(8,128)S(1)}, s32[8,32,8,128]{3,2,1,0:T(8,128)S(1)}) custom-call(f32[4,64,8,128]{3,2,1,0:T(8,128)S(1)} %get-tuple-element.12.viewed, s32[4,64,8,128]{3,2,1,0:T(8,128)S(1)} %get-tuple-element.13.materials), custom_call_target="tpu_custom_call" | custom-call | tf_op jit(solution)/shard_map/pallas_call | solution.py:375
  31.6 0.0 copy-done.2
  31.6 0.0 copy-done.4
  31.7 8.9 %shard_map.57 = (f32[4,32,8,128]{3,2,1,0:T(8,128)S(1)}, f32[24,32,8,128]{3,2,1,0:T(8,128)S(1)}, f32[8,8,128]{2,1,0:T(8,128)S(1)}) custom-call(f32[12,36,8,128]{3,2,1,0:T(8,128)S(1)} %get-tuple-element.14.volume, s32[8,32,8,128]{3,2,1,0:T(8,128)S(1)} %get-tuple-element.15.labels, f32[16]{0:T(128)S(1)} %copy-done.4, f32[3,16]{1,0:T(4,128)S(1)} %copy-done.2), custom_call_target="tpu_custom_call" | custom-call | tf_op jit(solution)/shard_map/pallas_call | solution.py:144
  40.6 19.7 %shard_map.58 = f32[4,4,8,128]{3,2,1,0:T(8,128)S(1)} custom-call(f32[4,32,8,128]{3,2,1,0:T(8,128)S(1)} %get-tuple-element.16.plain, f32[24,32,8,128]{3,2,1,0:T(8,128)S(1)} %get-tuple-element.17.lit, f32[8,8,128]{2,1,0:T(8,128)S(1)} %get-tuple-element.18.through), custom_call_target="tpu_custom_call" | custom-call | tf_op jit(solution)/shard_map/pallas_call | solution.py:600
  60.3 0.7 %copy.8 = f32[1,4,32,128]{3,1,2,0:T(4,128)} copy(f32[1,4,32,128]{3,2,1,0:T(8,128)S(1)} %bitcast.5) | data formatting | bytes 131072
Async XLA Ops:
  0.0 1.2 %copy-start = (f32[4,64,1024]{2,1,0:T(8,128)S(1)}, f32[4,64,1024]{2,1,0:T(8,128)}, u32[]{:S(2)}) copy-start(f32[4,64,1024]{2,1,0:T(8,128)} %density.1) | copy-start | bytes 3145732
  1.2 1.2 %copy-start.1 = (s32[4,64,1024]{2,1,0:T(8,128)S(1)}, s32[4,64,1024]{2,1,0:T(8,128)}, u32[]{:S(2)}) copy-start(s32[4,64,1024]{2,1,0:T(8,128)} %labels.1) | copy-start | bytes 3145732
  2.5 0.7 %copy-start.3 = (s32[4]{0:T(128)S(1)}, s32[4]{0:T(128)}, u32[]{:S(2)}) copy-start(s32[4]{0:T(128)} %order.1) | copy-start | bytes 52
  3.1 28.5 %copy-start.2 = (f32[3,16]{1,0:T(4,128)S(1)}, f32[3,16]{1,0:T(4,128)}, u32[]{:S(2)}) copy-start(f32[3,16]{1,0:T(4,128)} %albedo.1) | copy-start | bytes 580
  3.1 28.5 %copy-start.4 = (f32[16]{0:T(128)S(1)}, f32[16]{0:T(128)}, u32[]{:S(2)}) copy-start(f32[16]{0:T(128)} %extinction.1) | copy-start | bytes 196

commit v4 on v3

--- a/solution.py
+++ b/solution.py
@@ -62,64 +62,24 @@
     return jnp.take_along_axis(table, index, axis=1, mode="promise_in_bounds")
 
 
-def shade_kernel(depth_count, light_count, volume, labels, extinction, albedo, plain, lit, through, smooth):
+def shade_kernel(heat, turned, labels, extinction, albedo, plain, lit, through):
     slices, rows = labels.shape[:2]
-    depth_at = lax.axis_index("depth")
-    light_at = lax.axis_index("light")
-    pair_at = depth_at // 2
-    stripe_at = light_at * 2 + depth_at % 2
     lane = lax.broadcasted_iota(jnp.int32, (SUB, LANE), 1)
-    sub = lax.broadcasted_iota(jnp.int32, (SUB, LANE), 0)
-    first = (lane == 0) & (sub == 0)
-    last = (lane == LANE - 1) & (sub == SUB - 1)
     tables = [jnp.zeros((SUB, LANE), jnp.float32) for _ in range(4)]
     for k in range(extinction.shape[0]):
         tables[0] = jnp.where(lane == k, extinction[k], tables[0])
         for c in range(3):
             tables[c + 1] = jnp.where(lane == k, albedo[c, k], tables[c + 1])
-    has_below = (pair_at > 0).astype(jnp.float32)
-    has_above = (pair_at < depth_count // 2 - 1).astype(jnp.float32)
-    has_before = (stripe_at > 0).astype(jnp.float32)
-    has_after = (stripe_at < 2 * light_count - 1).astype(jnp.float32)
-
-    def cell(z, row):
-        return volume[z + 2, row]
-
-    def smooth_row(i, carry):
-        column = [cell(z, i + 1) for z in range(-2, slices + 2)]
-        for z in range(-1, slices + 1):
-            center = column[z + 2]
-            low, high = beside_y(center, lane, first, last)
-            total = (column[z + 1] + column[z + 3]) + (cell(z, i) + cell(z, i + 2)) + (low + high)
-            value = 0.4 * center + 0.1 * total
-            if z < 0:
-                value = value * has_below
-            if z >= slices:
-                value = value * has_above
-            smooth[z + 1, i] = value
-        return carry
-
-    lax.fori_loop(0, rows + 2, smooth_row, 0)
-    for z in range(slices):
-        smooth[z + 1, 0] = smooth[z + 1, 0] * has_before
-        smooth[z + 1, rows + 1] = smooth[z + 1, rows + 1] * has_after
-
     def shade_row(r, lights):
         lights = list(lights)
         remaining = jnp.ones((SUB, LANE), jnp.float32)
         flat = [jnp.zeros((SUB, LANE), jnp.float32) for _ in range(3)]
         for z in range(slices):
-            center = smooth[z + 1, r + 1]
-            low, high = beside_y(center, lane, first, last)
-            grad_z = smooth[z + 2, r + 1] - smooth[z, r + 1]
-            grad_x = smooth[z + 1, r + 2] - smooth[z + 1, r]
-            grad_y = high - low
-            facing = grad_x * lax.rsqrt(grad_z * grad_z + grad_x * grad_x + grad_y * grad_y + 0.2)
             index = labels[z, r]
-            optical = lookup(tables[0], index) * jnp.exp(center)
+            optical = lookup(tables[0], index) * heat[z, r]
             passed = jnp.exp(-optical)
             weight = (1.0 - passed) * remaining
-            glow = weight * lights[z] * (0.5 + 0.5 * facing)
+            glow = weight * lights[z] * turned[z, r]
             faint = 0.2 * weight
             for c in range(3):
                 tint = lookup(tables[c + 1], index)
@@ -138,21 +98,20 @@
         through[z] = lights[z]
 
 
-def shade(volume, labels, extinction, albedo, depth_count, light_count):
+def shade(heat, turned, labels, extinction, albedo):
     slices, rows = labels.shape[:2]
     f32 = jnp.float32
     return pl.pallas_call(
-        functools.partial(shade_kernel, depth_count, light_count),
-        in_specs=[VMEM_SPEC] * 2 + [pl.BlockSpec(memory_space=pltpu.SMEM)] * 2,
+        shade_kernel,
+        in_specs=[VMEM_SPEC] * 3 + [pl.BlockSpec(memory_space=pltpu.SMEM)] * 2,
         out_specs=[VMEM_SPEC] * 3,
         out_shape=[
             jax.ShapeDtypeStruct((4, rows, SUB, LANE), f32),
             jax.ShapeDtypeStruct((slices * 3, rows, SUB, LANE), f32),
             jax.ShapeDtypeStruct((slices, SUB, LANE), f32),
         ],
-        scratch_shapes=[pltpu.VMEM((slices + 2, rows + 2, SUB, LANE), f32)],
         compiler_params=pltpu.CompilerParams(vmem_limit_bytes=40 * 1024 * 1024),
-    )(volume, labels, extinction, albedo)
+    )(heat, turned, labels, extinction, albedo)
 
 
 def greet(wanted):
@@ -168,7 +127,48 @@
     pl.semaphore_wait(barrier, count)
 
 
-def trade_kernel(depth_count, light_count, viewed, materials, volume, labels, local_sem, send_sem, recv_sem):
+def slopes(volume, smooth, heat, turned, flags):
+    slices, rows = heat.shape[:2]
+    lane = lax.broadcasted_iota(jnp.int32, (SUB, LANE), 1)
+    sub = lax.broadcasted_iota(jnp.int32, (SUB, LANE), 0)
+    first = (lane == 0) & (sub == 0)
+    last = (lane == LANE - 1) & (sub == SUB - 1)
+
+    def smooth_row(i, carry):
+        column = [volume[z, i + 1] for z in range(slices + 4)]
+        for z in range(slices + 2):
+            center = column[z + 1]
+            low, high = beside_y(center, lane, first, last)
+            total = (column[z] + column[z + 2]) + (volume[z + 1, i] + volume[z + 1, i + 2]) + (low + high)
+            value = 0.4 * center + 0.1 * total
+            if z == 0:
+                value = value * flags[0]
+            if z == slices + 1:
+                value = value * flags[1]
+            smooth[z, i] = value
+        return carry
+
+    lax.fori_loop(0, rows + 2, smooth_row, 0)
+    for z in range(slices):
+        smooth[z + 1, 0] = smooth[z + 1, 0] * flags[2]
+        smooth[z + 1, rows + 1] = smooth[z + 1, rows + 1] * flags[3]
+
+    def slope_row(r, carry):
+        for z in range(slices):
+            center = smooth[z + 1, r + 1]
+            low, high = beside_y(center, lane, first, last)
+            grad_z = smooth[z + 2, r + 1] - smooth[z, r + 1]
+            grad_x = smooth[z + 1, r + 2] - smooth[z + 1, r]
+            grad_y = high - low
+            facing = grad_x * lax.rsqrt(grad_z * grad_z + grad_x * grad_x + grad_y * grad_y + 0.2)
+            heat[z, r] = jnp.exp(center)
+            turned[z, r] = 0.5 + 0.5 * facing
+        return carry
+
+    lax.fori_loop(0, rows, slope_row, 0)
+
+
+def trade_kernel(depth_count, light_count, viewed, materials, heat, turned, labels, volume, smooth, local_sem, send_sem, recv_sem):
     slices, rows = viewed.shape[:2]
     half = rows // 2
     depth_at = lax.axis_index("depth")
@@ -338,16 +338,19 @@
     def _():
         swaps[1].wait_recv()
 
+    @pl.when(has_above)
+    def _():
+        below.wait_recv()
+
+    @pl.when(has_below)
+    def _():
+        above.wait_recv()
+
+    stripe = light_at * 2 + side
+    flags = [has_below, has_above, stripe > 0, stripe < 2 * light_count - 1]
+    slopes(volume, smooth, heat, turned, [jnp.where(flag, 1.0, 0.0) for flag in flags])
     swaps[2].wait_recv()
     keep_labels.wait()
-
-    @pl.when(has_above)
-    def _():
-        below.wait_recv()
-
-    @pl.when(has_below)
-    def _():
-        above.wait_recv()
 
     for one in swaps:
         one.wait_send()
@@ -375,12 +378,15 @@
     return pl.pallas_call(
         functools.partial(trade_kernel, depth_count, light_count),
         in_specs=[VMEM_SPEC] * 2,
-        out_specs=[VMEM_SPEC] * 2,
+        out_specs=[VMEM_SPEC] * 3,
         out_shape=[
-            jax.ShapeDtypeStruct((2 * slices + 4, half + 4, SUB, LANE), jnp.float32),
+            jax.ShapeDtypeStruct((2 * slices, half, SUB, LANE), jnp.float32),
+            jax.ShapeDtypeStruct((2 * slices, half, SUB, LANE), jnp.float32),
             jax.ShapeDtypeStruct((2 * slices, half, SUB, LANE), jnp.int32),
         ],
         scratch_shapes=[
+            pltpu.VMEM((2 * slices + 4, half + 4, SUB, LANE), jnp.float32),
+            pltpu.VMEM((2 * slices + 2, half + 2, SUB, LANE), jnp.float32),
             pltpu.SemaphoreType.DMA((2,)),
             pltpu.SemaphoreType.DMA((7,)),
             pltpu.SemaphoreType.DMA((7,)),
@@ -614,8 +620,8 @@
     light_count = lax.axis_size("light")
     slices, rows, columns = density.shape
     viewed, materials = reorder(density, labels, slice_order)
-    volume, stripe_labels = trade(viewed, materials, depth_count, light_count)
-    plain, lit, through = shade(volume, stripe_labels, extinction, albedo, depth_count, light_count)
+    heat, turned, stripe_labels = trade(viewed, materials, depth_count, light_count)
+    plain, lit, through = shade(heat, turned, stripe_labels, extinction, albedo)
     return merge(plain, lit, through, depth_count, light_count).reshape(4, -1)
 
 

time: 61.2 us -> 57.2 us (0.935)
  Pallas kernels: 57.2 us -> 53.2 us
    pallas_call x1, Pallas kernels: 8.93 us -> 4.98 us  [shade(): pl.pallas_call(shade_kernel, in_specs=[VMEM_SPEC] * 3 + [pl.BlockSpec(mem...]
where the time goes in v4:
time: 57.2 us; the launch traced here: 57 us
  Pallas kernels  53.2 us (93%)
  local copies, waits for them, and re-layouts  3.78 us (7%)
    pallas_call x1, Pallas kernels, trade(): pl.pallas_call(functools.partial(trade_kernel, depth_count, light_count),...  27.3 us
    pallas_call x1, Pallas kernels, merge(): pl.pallas_call(functools.partial(merge_kernel, depth_count, light_count),...  19.7 us
    pallas_call x1, Pallas kernels, shade(): pl.pallas_call(shade_kernel, in_specs=[VMEM_SPEC] * 3 + [pl.BlockSpec(mem...  4.98 us
    unnamed x11, local copies, waits for them, and re-layouts  3.78 us
    pallas_call x1, Pallas kernels, reorder(): pl.pallas_call(reorder_kernel, in_specs=[pl.BlockSpec(memory_space=pltpu....  1.25 us

profile of v4, /device:TPU:24, one launch (start us, length us, event | category | flops | bytes accessed | tf_op | source)
XLA Modules:
  0.0 57.0 jit_solution(8356237179192618854)
XLA Ops:
  0.0 0.0 copy-start
  0.0 1.2 %copy-done = f32[4,64,1024]{2,1,0:T(8,128)S(1)} copy-done((f32[4,64,1024]{2,1,0:T(8,128)S(1)}, f32[4,64,1024]{2,1,0:T(8,128)}, u32[]{:S(2)}) %copy-start) | copy-done | bytes 1048600
  1.2 0.0 copy-start.1
  1.2 1.2 %copy-done.1 = s32[4,64,1024]{2,1,0:T(8,128)S(1)} copy-done((s32[4,64,1024]{2,1,0:T(8,128)S(1)}, s32[4,64,1024]{2,1,0:T(8,128)}, u32[]{:S(2)}) %copy-start.1) | copy-done | bytes 1048600
  2.5 0.0 copy-start.3
  2.5 0.7 %copy-done.3 = s32[4]{0:T(128)S(1)} copy-done((s32[4]{0:T(128)S(1)}, s32[4]{0:T(128)}, u32[]{:S(2)}) %copy-start.3) | copy-done | bytes 40
  3.1 0.0 copy-start.2
  3.1 0.0 copy-start.4
  3.1 1.3 %shard_map.55 = (f32[4,64,8,128]{3,2,1,0:T(8,128)S(1)}, s32[4,64,8,128]{3,2,1,0:T(8,128)S(1)}) custom-call(s32[4]{0:T(128)S(1)} %copy-done.3, f32[4,64,1024]{2,1,0:T(8,128)S(1)} %copy-done, s32[4,64,1024]{2,1,0:T(8,128)S(1)} %copy-done.1), custom_call_target="tpu_custom_call" | custom-call | tf_op jit(solution)/shard_map/pallas_call | solution.py:36
  4.4 27.3 %shard_map.56 = (f32[8,32,8,128]{3,2,1,0:T(8,128)S(1)}, f32[8,32,8,128]{3,2,1,0:T(8,128)S(1)}, s32[8,32,8,128]{3,2,1,0:T(8,128)S(1)}) custom-call(f32[4,64,8,128]{3,2,1,0:T(8,128)S(1)} %get-tuple-element.13.viewed, s32[4,64,8,128]{3,2,1,0:T(8,128)S(1)} %get-tuple-element.14.materials), custom_call_target="tpu_custom_call" | custom-call | tf_op jit(solution)/shard_map/pallas_call | solution.py:378
  31.6 0.0 copy-done.2
  31.6 0.0 copy-done.4
  31.7 5.0 %shard_map.57 = (f32[4,32,8,128]{3,2,1,0:T(8,128)S(1)}, f32[24,32,8,128]{3,2,1,0:T(8,128)S(1)}, f32[8,8,128]{2,1,0:T(8,128)S(1)}) custom-call(f32[8,32,8,128]{3,2,1,0:T(8,128)S(1)} %get-tuple-element.15.heat, f32[8,32,8,128]{3,2,1,0:T(8,128)S(1)} %get-tuple-element.16.turned, s32[8,32,8,128]{3,2,1,0:T(8,128)S(1)} %get-tuple-element.17.labels, ...), custom_call_target="tpu_custom_call" | custom-call | tf_op jit(solution)/shard_map/pallas_call | solution.py:104
  36.6 19.7 %shard_map.58 = f32[4,4,8,128]{3,2,1,0:T(8,128)S(1)} custom-call(f32[4,32,8,128]{3,2,1,0:T(8,128)S(1)} %get-tuple-element.18.plain, f32[24,32,8,128]{3,2,1,0:T(8,128)S(1)} %get-tuple-element.19.lit, f32[8,8,128]{2,1,0:T(8,128)S(1)} %get-tuple-element.20.through), custom_call_target="tpu_custom_call" | custom-call | tf_op jit(solution)/shard_map/pallas_call | solution.py:606
  56.4 0.7 %copy.8 = f32[1,4,32,128]{3,1,2,0:T(4,128)} copy(f32[1,4,32,128]{3,2,1,0:T(8,128)S(1)} %bitcast.5) | data formatting | bytes 131072
Async XLA Ops:
  0.0 1.2 %copy-start = (f32[4,64,1024]{2,1,0:T(8,128)S(1)}, f32[4,64,1024]{2,1,0:T(8,128)}, u32[]{:S(2)}) copy-start(f32[4,64,1024]{2,1,0:T(8,128)} %density.1) | copy-start | bytes 3145732
  1.2 1.2 %copy-start.1 = (s32[4,64,1024]{2,1,0:T(8,128)S(1)}, s32[4,64,1024]{2,1,0:T(8,128)}, u32[]{:S(2)}) copy-start(s32[4,64,1024]{2,1,0:T(8,128)} %labels.1) | copy-start | bytes 3145732
  2.5 0.7 %copy-start.3 = (s32[4]{0:T(128)S(1)}, s32[4]{0:T(128)}, u32[]{:S(2)}) copy-start(s32[4]{0:T(128)} %order.1) | copy-start | bytes 52
  3.1 28.5 %copy-start.2 = (f32[3,16]{1,0:T(4,128)S(1)}, f32[3,16]{1,0:T(4,128)}, u32[]{:S(2)}) copy-start(f32[3,16]{1,0:T(4,128)} %albedo.1) | copy-start | bytes 580
  3.1 28.5 %copy-start.4 = (f32[16]{0:T(128)S(1)}, f32[16]{0:T(128)}, u32[]{:S(2)}) copy-start(f32[16]{0:T(128)} %extinction.1) | copy-start | bytes 196

commit v5 on v4

--- a/solution.py
+++ b/solution.py
@@ -47,7 +47,11 @@
             pltpu.SemaphoreType.DMA((2 * slices,)),
         ],
         compiler_params=pltpu.CompilerParams(vmem_limit_bytes=12 * 1024 * 1024),
-    )(order, density, labels)
+    )(
+        order,
+        pltpu.with_memory_space_constraint(density, pltpu.HBM),
+        pltpu.with_memory_space_constraint(labels, pltpu.HBM),
+    )
 
 
 def beside_y(cells, lane, first, last):

time: 57.2 us -> 55.7 us (0.974)
  local copies, waits for them, and re-layouts: 3.78 us -> 1.35 us
  Pallas kernels: 53.2 us -> 54.1 us
    unnamed x11 -> x7, local copies, waits for them, and re-layouts: 3.78 us -> 1.35 us
    pallas_call x1, Pallas kernels: 1.25 us -> 2.18 us  [reorder(): pl.pallas_call(reorder_kernel, in_specs=[pl.BlockSpec(memory_space=pltpu....]
where the time goes in v5:
time: 55.7 us; the launch traced here: 55.5 us
  Pallas kernels  54.1 us (97%)
  local copies, waits for them, and re-layouts  1.35 us (2%)
    pallas_call x1, Pallas kernels, trade(): pl.pallas_call(functools.partial(trade_kernel, depth_count, light_count),...  27.3 us
    pallas_call x1, Pallas kernels, merge(): pl.pallas_call(functools.partial(merge_kernel, depth_count, light_count),...  19.7 us
    pallas_call x1, Pallas kernels, shade(): pl.pallas_call(shade_kernel, in_specs=[VMEM_SPEC] * 3 + [pl.BlockSpec(mem...  4.98 us
    pallas_call x1, Pallas kernels, reorder(): pl.pallas_call(reorder_kernel, in_specs=[pl.BlockSpec(memory_space=pltpu....  2.18 us
    unnamed x7, local copies, waits for them, and re-layouts  1.35 us

profile of v5, /device:TPU:24, one launch (start us, length us, event | category | flops | bytes accessed | tf_op | source)
XLA Modules:
  0.0 55.5 jit_solution(5564239788199726656)
XLA Ops:
  0.0 0.0 copy-start
  0.0 0.0 copy-start.1
  0.0 0.7 %copy-done.1 = s32[4]{0:T(128)S(1)} copy-done((s32[4]{0:T(128)S(1)}, s32[4]{0:T(128)}, u32[]{:S(2)}) %copy-start.1) | copy-done | bytes 40
  0.7 0.0 copy-start.2
  0.7 2.2 %shard_map.55 = (f32[4,64,8,128]{3,2,1,0:T(8,128)S(1)}, s32[4,64,8,128]{3,2,1,0:T(8,128)S(1)}) custom-call(s32[4]{0:T(128)S(1)} %copy-done.1, f32[4,64,1024]{2,1,0:T(8,128)} %density.1, s32[4,64,1024]{2,1,0:T(8,128)} %labels.1), custom_call_target="tpu_custom_call" | custom-call | tf_op jit(solution)/shard_map/pallas_call | solution.py:36
  2.9 27.3 %shard_map.56 = (f32[8,32,8,128]{3,2,1,0:T(8,128)S(1)}, f32[8,32,8,128]{3,2,1,0:T(8,128)S(1)}, s32[8,32,8,128]{3,2,1,0:T(8,128)S(1)}) custom-call(f32[4,64,8,128]{3,2,1,0:T(8,128)S(1)} %get-tuple-element.13.viewed, s32[4,64,8,128]{3,2,1,0:T(8,128)S(1)} %get-tuple-element.14.materials), custom_call_target="tpu_custom_call" | custom-call | tf_op jit(solution)/shard_map/pallas_call | solution.py:382
  30.1 0.0 copy-done
  30.1 0.0 copy-done.2
  30.1 5.0 %shard_map.57 = (f32[4,32,8,128]{3,2,1,0:T(8,128)S(1)}, f32[24,32,8,128]{3,2,1,0:T(8,128)S(1)}, f32[8,8,128]{2,1,0:T(8,128)S(1)}) custom-call(f32[8,32,8,128]{3,2,1,0:T(8,128)S(1)} %get-tuple-element.15.heat, f32[8,32,8,128]{3,2,1,0:T(8,128)S(1)} %get-tuple-element.16.turned, s32[8,32,8,128]{3,2,1,0:T(8,128)S(1)} %get-tuple-element.17.labels, ...), custom_call_target="tpu_custom_call" | custom-call | tf_op jit(solution)/shard_map/pallas_call | solution.py:108
  35.1 19.7 %shard_map.58 = f32[4,4,8,128]{3,2,1,0:T(8,128)S(1)} custom-call(f32[4,32,8,128]{3,2,1,0:T(8,128)S(1)} %get-tuple-element.18.plain, f32[24,32,8,128]{3,2,1,0:T(8,128)S(1)} %get-tuple-element.19.lit, f32[8,8,128]{2,1,0:T(8,128)S(1)} %get-tuple-element.20.through), custom_call_target="tpu_custom_call" | custom-call | tf_op jit(solution)/shard_map/pallas_call | solution.py:610
  54.8 0.7 %copy.8 = f32[1,4,32,128]{3,1,2,0:T(4,128)} copy(f32[1,4,32,128]{3,2,1,0:T(8,128)S(1)} %bitcast.5) | data formatting | bytes 131072
Async XLA Ops:
  0.0 30.1 %copy-start = (f32[3,16]{1,0:T(4,128)S(1)}, f32[3,16]{1,0:T(4,128)}, u32[]{:S(2)}) copy-start(f32[3,16]{1,0:T(4,128)} %albedo.1) | copy-start | bytes 580
  0.0 0.7 %copy-start.1 = (s32[4]{0:T(128)S(1)}, s32[4]{0:T(128)}, u32[]{:S(2)}) copy-start(s32[4]{0:T(128)} %order.1) | copy-start | bytes 52
  0.7 29.5 %copy-start.2 = (f32[16]{0:T(128)S(1)}, f32[16]{0:T(128)}, u32[]{:S(2)}) copy-start(f32[16]{0:T(128)} %extinction.1) | copy-start | bytes 196
